TPU v7x, 32 devices: a whole 2x2x4 slice. The times are simulated.
32 devices in a mesh: view: 2 (over core), gz: 8 (over z, y), gy: 2 (over x).
Axes of the slice: x: 2, y: 2, z: 4, core: 2. Of those that a mesh axis runs over, the one named last changes fastest.
Arguments:
- observed: float32 [2, 512, 32, 256], P('view', 'gz', 'gy'), may hold values from 0.5 to 4
- start: float32 [512, 32, 256], P('gz', 'gy'), may hold values from 0.5 to 2
- spread_z: float32 [2, 31], P('view'), may hold values from 0.05 to 1
- spread_y: float32 [2, 7], P('view'), may hold values from 0.1 to 1
- spread_x: float32 [2, 7], P('view'), may hold values from 0.1 to 1
Outputs:
- estimate: float32 [512, 32, 256], P('gz', 'gy')
All inputs are finite; a program needn't handle non-finite values.
Results may differ from a plain program's by a relative error of at most 0.0001.
Values sent between devices are 32-bit elements; how exact they have to be, the bound alone decides.
A program may use at most 64 MiB of HBM per device.

v0:
```python
import jax
import jax.numpy as jnp
from jax import lax
from jax.sharding import PartitionSpec as P

KZ = 31
KY = 7
KX = 7
ITERS = 2


def padded_2(x, sides, width):
    for axis, dim in sides:
        peers, length = (lax.axis_size(axis), x.shape[dim])
        up = [(i, (i + 1) % peers) for i in range(peers - 1)]
        down = [(j, i) for i, j in up]
        last = lax.slice_in_dim(x, length - width, length, axis=dim)
        first = lax.slice_in_dim(x, 0, width, axis=dim)
        before = lax.ppermute(last, axis, up)
        after = lax.ppermute(first, axis, down)
        x = jnp.concatenate([before, x, after], axis=dim)
    return x


def correlate(field, weights, along, margin):
    padding = [(0, 0), (0, 0), (0, 0)]
    padding[along] = (margin, margin)
    padded = jnp.pad(field, padding)
    taps = weights.shape[0]
    length = padded.shape[along] - taps + 1
    total = weights[0] * lax.slice_in_dim(padded, 0, length, 1, along)
    for offset in range(1, taps):
        total = total + weights[offset] * lax.slice_in_dim(
            padded, offset, offset + length, 1, along
        )
    return total


def blur_local(field, weight_z, weight_y, weight_x):
    padded = padded_2(field, (("gz", 0),), KZ // 2)
    field = correlate(padded, weight_z, 0, 0)
    padded = padded_2(field, (("gy", 1),), KY // 2)
    field = correlate(padded, weight_y, 1, 0)
    return correlate(field, weight_x, 2, KX // 2)


def on_device(observed, start, spread_z, spread_y, spread_x):
    recorded = observed[0]
    weight_z = spread_z[0] / jnp.sum(spread_z[0])
    weight_y = spread_y[0] / jnp.sum(spread_y[0])
    weight_x = spread_x[0] / jnp.sum(spread_x[0])
    estimate = start
    for sweep in range(ITERS):
        blurred = blur_local(estimate, weight_z, weight_y, weight_x)
        quotient = recorded / blurred
        correction = blur_local(quotient, weight_z[::-1], weight_y[::-1], weight_x[::-1])
        summed = lax.psum(correction, "view")
        estimate = estimate * (0.5 * summed)
    return estimate


def solution(mesh):
    return jax.shard_map(
        on_device,
        mesh=mesh,
        in_specs=(
            P("view", "gz", "gy", None),
            P("gz", "gy", None),
            P("view", None),
            P("view", None),
            P("view", None),
        ),
        out_specs=P("gz", "gy", None),
        check_vma=False,
    )
```

profile of v0, /device:TPU:19, one launch (start us, length us, event | category | flops | bytes accessed | tf_op | source)
XLA Modules:
  0.0 311.1 jit_solution(4010163259082128187)
XLA Ops:
  6.5 1.2 fusion.415
  7.7 3.1 %collective-permute-start = (f32[15,16,256]{2,1,0:T(8,128)S(1)}, f32[15,16,256]{2,1,0:T(8,128)S(1)}, u32[]{:S(2)}, u32[]{:S(2)}) collective-permute-start(f32[15,16,256]{2,1,0:T(8,128)S(1)} %get-tuple-element.21), channel_id=1, source_target_pairs={{0,2},{2,4},{4,6},{6,8},{8,10},{10,12},{12,14},{1,3},{3,5},{5,7},{... | collective-permute-start | bytes 737288 | tf_op jit(solution)/shard_map/ppermute | solution.py:19
  10.9 3.0 collective-permute-start.1
  13.9 1.3 reduce_sum.29
  15.2 0.7 reverse.11
  15.9 1.3 broadcast_divide_fusion
  17.2 0.7 fusion.422
  18.0 1.3 reduce_sum.28
  19.2 0.7 reverse.10
  20.0 1.3 broadcast_divide_fusion.2
  21.3 0.7 fusion.423
  22.0 1.3 reduce_sum.27
  23.2 0.7 reverse.9
  24.0 1.3 broadcast_divide_fusion.4
  25.3 0.3 constant_dynamic-update-slice_fusion
  25.6 23.5 %fusion.378 = f32[64,16,256]{2,1,0:T(8,128)S(1)} fusion(f32[79,16,256]{2,1,0:T(8,128)S(1)} %constant_dynamic-update-slice_fusion.2, f32[79,16,256]{2,1,0:T(8,128)S(1)} %get-tuple-element.19, f32[64,16,256]{2,1,0:T(8,128)S(1)} %copy-done, f32[]{:T(128)} %bitcast.39, f32[]{:T(128)} %bitcast.38, f32[]{:T(128)} %bitcast.37, f32[]{:T(128)} %bitcast.36, ...), kind=kLoop, calls=%fused_computation.617 | loop fusion | flops 15990784 | bytes 33554556 | tf_op jit(solution)/shard_map/add | solution.py:33
  49.3 2.2 collective-permute-start.3
  51.5 1.3 collective-permute-start.2
  52.8 0.7 fusion.421
  53.4 0.7 fusion.420
  54.1 1.7 collective-permute-done.3
  55.9 3.8 %collective-permute-done.2 = f32[64,3,256]{2,1,0:T(4,128)S(1)} collective-permute-done((f32[64,3,256]{2,1,0:T(4,128)S(1)}, f32[64,3,256]{2,1,0:T(4,128)S(1)}, u32[]{:S(2)}, u32[]{:S(2)}) %collective-permute-start.2) | collective-permute-done | bytes 196640 | tf_op jit(solution)/shard_map/ppermute | solution.py:19
  59.7 5.4 %fusion.45 = f32[64,16,256]{2,1,0:T(8,128)S(1)} fusion(f32[64,16,256]{2,1,0:T(8,128)S(1)} %fusion.378, f32[64,3,256]{2,1,0:T(4,128)S(1)} %collective-permute-done.3, f32[64,3,256]{2,1,0:T(4,128)S(1)} %collective-permute-done.2, f32[]{:T(128)} %bitcast.45, f32[]{:T(128)} %bitcast.44, f32[]{:T(128)} %bitcast.43, f32[]{:T(128)} %bitcast.42, f32[]{:T(128)} %bitcast.41, ...), kind=kLoop, calls=%fused_computation.269 | loop fusion | flops 4980736 | bytes 2490396 | tf_op jit(solution)/shard_map/add | solution.py:33
  65.1 6.1 %fusion.321 = f32[64,16,256]{2,1,0:T(8,128)S(1)} fusion(f32[64,16,256]{2,1,0:T(8,128)S(1)} %fusion.45, f32[1,64,16,256]{3,2,1,0:T(8,128)S(1)} %copy-done.1, f32[]{:T(128)} %bitcast.51, f32[]{:T(128)} %bitcast.50, f32[]{:T(128)} %bitcast.49, f32[]{:T(128)} %bitcast.48, f32[]{:T(128)} %bitcast.47, f32[]{:T(128)} %bitcast.46, f32[]{:T(128)} %bitcast.7), kind=kLoop, calls=%fused_computation.545 | loop fusion | flops 3670016 | bytes 3145756 | tf_op jit(solution)/shard_map/div | solution.py:55
  71.3 2.1 collective-permute-start.5
  73.4 3.1 %collective-permute-start.4 = (f32[15,16,256]{2,1,0:T(8,128)S(1)}, f32[15,16,256]{2,1,0:T(8,128)S(1)}, u32[]{:S(2)}, u32[]{:S(2)}) collective-permute-start(f32[15,16,256]{2,1,0:T(8,128)S(1)} %get-tuple-element.15), channel_id=1, source_target_pairs={{0,2},{2,4},{4,6},{6,8},{8,10},{10,12},{12,14},{1,3},{3,5},{5,7},{... | collective-permute-start | bytes 737288 | tf_op jit(solution)/shard_map/ppermute | solution.py:19
  76.6 0.7 fusion.419
  77.3 0.7 fusion.418
  78.2 7.0 %collective-permute-done.4 = f32[15,16,256]{2,1,0:T(8,128)S(1)} collective-permute-done((f32[15,16,256]{2,1,0:T(8,128)S(1)}, f32[15,16,256]{2,1,0:T(8,128)S(1)}, u32[]{:S(2)}, u32[]{:S(2)}) %collective-permute-start.4) | collective-permute-done | bytes 245792 | tf_op jit(solution)/shard_map/ppermute | solution.py:19
  85.3 23.9 %fusion.231 = f32[64,16,256]{2,1,0:T(8,128)S(1)} fusion(f32[64,16,256]{2,1,0:T(8,128)S(1)} %fusion.321, f32[15,16,256]{2,1,0:T(8,128)S(1)} %collective-permute-done.5, f32[15,16,256]{2,1,0:T(8,128)S(1)} %collective-permute-done.4, f32[]{:T(128)} %bitcast.81, f32[]{:T(128)} %bitcast.80, f32[]{:T(128)} %bitcast.79, f32[]{:T(128)} %bitcast.78, f32[]{:T(128)} %bitcast.77, ...), kind=kLoop, calls=%fused_computation.455 | loop fusion | flops 23855104 | bytes 2588796 | tf_op jit(solution)/shard_map/add | solution.py:33
  109.3 1.3 collective-permute-start.7
  110.6 1.3 collective-permute-start.6
  111.9 0.7 fusion.417
  112.6 0.6 fusion.416
  113.2 1.4 collective-permute-done.7
  114.6 3.8 %collective-permute-done.6 = f32[64,3,256]{2,1,0:T(4,128)S(1)} collective-permute-done((f32[64,3,256]{2,1,0:T(4,128)S(1)}, f32[64,3,256]{2,1,0:T(4,128)S(1)}, u32[]{:S(2)}, u32[]{:S(2)}) %collective-permute-start.6) | collective-permute-done | bytes 196640 | tf_op jit(solution)/shard_map/ppermute | solution.py:19
  118.4 5.4 %fusion.31 = f32[64,16,256]{2,1,0:T(8,128)S(1)} fusion(f32[64,16,256]{2,1,0:T(8,128)S(1)} %fusion.231, f32[64,3,256]{2,1,0:T(4,128)S(1)} %collective-permute-done.7, f32[64,3,256]{2,1,0:T(4,128)S(1)} %collective-permute-done.6, f32[]{:T(128)} %bitcast.87, f32[]{:T(128)} %bitcast.86, f32[]{:T(128)} %bitcast.85, f32[]{:T(128)} %bitcast.84, f32[]{:T(128)} %bitcast.83, ...), kind=kLoop, calls=%fused_computation.255 | loop fusion | flops 4980736 | bytes 2490396 | tf_op jit(solution)/shard_map/add | solution.py:33
  123.9 6.8 %fusion.333 = f32[64,16,256]{2,1,0:T(8,128)} fusion(f32[64,16,256]{2,1,0:T(8,128)S(1)} %fusion.31, f32[]{:T(128)} %bitcast.93, f32[]{:T(128)} %bitcast.92, f32[]{:T(128)} %bitcast.91, f32[]{:T(128)} %bitcast.90, f32[]{:T(128)} %bitcast.89, f32[]{:T(128)} %bitcast.88, f32[]{:T(128)} %bitcast.1), kind=kLoop, calls=%fused_computation.557 | loop fusion | flops 3407872 | bytes 2097180 | tf_op jit(solution)/shard_map/add | solution.py:33
  130.8 23.3 %all-reduce.7.cloned.1.call-done = f32[64,16,256]{2,1,0:T(8,128)} async-done(((f32[64,16,256]{2,1,0:T(8,128)}), f32[64,16,256]{2,1,0:T(8,128)}) %all-reduce.7.cloned.1.call-update) | async-done | bytes 1048592 | tf_op jit(solution)/shard_map/psum | solution.py:57
  154.1 1.4 multiply_multiply_fusion.1
  155.6 3.1 collective-permute-start.9
  158.7 2.4 collective-permute-start.8
  161.1 9.0 %collective-permute-done.9 = f32[15,16,256]{2,1,0:T(8,128)S(1)} collective-permute-done((f32[15,16,256]{2,1,0:T(8,128)S(1)}, f32[15,16,256]{2,1,0:T(8,128)S(1)}, u32[]{:S(2)}, u32[]{:S(2)}) %collective-permute-start.9) | collective-permute-done | bytes 245792 | tf_op jit(solution)/shard_map/ppermute | solution.py:20
  170.0 0.5 collective-permute-done.8
  170.5 23.7 %fusion.145 = f32[64,16,256]{2,1,0:T(8,128)S(1)} fusion(f32[64,16,256]{2,1,0:T(8,128)S(1)} %multiply_multiply_fusion.1, f32[15,16,256]{2,1,0:T(8,128)S(1)} %collective-permute-done.9, f32[15,16,256]{2,1,0:T(8,128)S(1)} %collective-permute-done.8, f32[]{:T(128)} %bitcast.39, f32[]{:T(128)} %bitcast.38, f32[]{:T(128)} %bitcast.37, f32[]{:T(128)} %bitcast.36, ...), kind=kLoop, calls=%fused_computation.369 | loop fusion | flops 23855104 | bytes 2588796 | tf_op jit(solution)/shard_map/add | solution.py:33
  194.4 2.2 collective-permute-start.11
  196.6 1.3 collective-permute-start.10
  197.9 3.7 %collective-permute-done.11 = f32[64,3,256]{2,1,0:T(4,128)S(1)} collective-permute-done((f32[64,3,256]{2,1,0:T(4,128)S(1)}, f32[64,3,256]{2,1,0:T(4,128)S(1)}, u32[]{:S(2)}, u32[]{:S(2)}) %collective-permute-start.11) | collective-permute-done | bytes 196640 | tf_op jit(solution)/shard_map/ppermute | solution.py:20
  201.6 3.8 %collective-permute-done.10 = f32[64,3,256]{2,1,0:T(4,128)S(1)} collective-permute-done((f32[64,3,256]{2,1,0:T(4,128)S(1)}, f32[64,3,256]{2,1,0:T(4,128)S(1)}, u32[]{:S(2)}, u32[]{:S(2)}) %collective-permute-start.10) | collective-permute-done | bytes 196640 | tf_op jit(solution)/shard_map/ppermute | solution.py:19
  205.5 5.3 %fusion.17 = f32[64,16,256]{2,1,0:T(8,128)S(1)} fusion(f32[64,16,256]{2,1,0:T(8,128)S(1)} %fusion.145, f32[64,3,256]{2,1,0:T(4,128)S(1)} %collective-permute-done.11, f32[64,3,256]{2,1,0:T(4,128)S(1)} %collective-permute-done.10, f32[]{:T(128)} %bitcast.45, f32[]{:T(128)} %bitcast.44, f32[]{:T(128)} %bitcast.43, f32[]{:T(128)} %bitcast.42, f32[]{:T(128)} %bitcast.41, ...), kind=kLoop, calls=%fused_computation.241 | loop fusion | flops 4980736 | bytes 2490396 | tf_op jit(solution)/shard_map/add | solution.py:33
  210.8 6.1 %fusion.346 = f32[64,16,256]{2,1,0:T(8,128)S(1)} fusion(f32[64,16,256]{2,1,0:T(8,128)S(1)} %fusion.17, f32[1,64,16,256]{3,2,1,0:T(8,128)S(1)} %copy-done.1, f32[]{:T(128)} %bitcast.51, f32[]{:T(128)} %bitcast.50, f32[]{:T(128)} %bitcast.49, f32[]{:T(128)} %bitcast.48, f32[]{:T(128)} %bitcast.47, f32[]{:T(128)} %bitcast.46, f32[]{:T(128)} %bitcast.7), kind=kLoop, calls=%fused_computation.570 | loop fusion | flops 3670016 | bytes 3145756 | tf_op jit(solution)/shard_map/div | solution.py:55
  216.9 4.2 %collective-permute-start.13 = (f32[15,16,256]{2,1,0:T(8,128)S(1)}, f32[15,16,256]{2,1,0:T(8,128)S(1)}, u32[]{:S(2)}, u32[]{:S(2)}) collective-permute-start(f32[15,16,256]{2,1,0:T(8,128)S(1)} %get-tuple-element.8), channel_id=1, source_target_pairs={{2,0},{4,2},{6,4},{8,6},{10,8},{12,10},{14,12},{3,1},{5,3},{7,5},{... | collective-permute-start | bytes 737288 | tf_op jit(solution)/shard_map/ppermute | solution.py:20
  221.2 1.9 collective-permute-start.12
  223.1 2.8 collective-permute-done.13
  225.9 7.1 %collective-permute-done.12 = f32[15,16,256]{2,1,0:T(8,128)S(1)} collective-permute-done((f32[15,16,256]{2,1,0:T(8,128)S(1)}, f32[15,16,256]{2,1,0:T(8,128)S(1)}, u32[]{:S(2)}, u32[]{:S(2)}) %collective-permute-start.12) | collective-permute-done | bytes 245792 | tf_op jit(solution)/shard_map/ppermute | solution.py:19
  233.0 23.9 %fusion.59 = f32[64,16,256]{2,1,0:T(8,128)S(1)} fusion(f32[64,16,256]{2,1,0:T(8,128)S(1)} %fusion.346, f32[15,16,256]{2,1,0:T(8,128)S(1)} %collective-permute-done.13, f32[15,16,256]{2,1,0:T(8,128)S(1)} %collective-permute-done.12, f32[]{:T(128)} %bitcast.81, f32[]{:T(128)} %bitcast.80, f32[]{:T(128)} %bitcast.79, f32[]{:T(128)} %bitcast.78, f32[]{:T(128)} %bitcast.77, ...), kind=kLoop, calls=%fused_computation.283 | loop fusion | flops 23855104 | bytes 2588796 | tf_op jit(solution)/shard_map/add | solution.py:33
  257.0 1.3 collective-permute-start.15
  258.3 1.3 collective-permute-start.14
  259.6 4.0 %collective-permute-done.15 = f32[64,3,256]{2,1,0:T(4,128)S(1)} collective-permute-done((f32[64,3,256]{2,1,0:T(4,128)S(1)}, f32[64,3,256]{2,1,0:T(4,128)S(1)}, u32[]{:S(2)}, u32[]{:S(2)}) %collective-permute-start.15) | collective-permute-done | bytes 196640 | tf_op jit(solution)/shard_map/ppermute | solution.py:20
  263.6 3.8 %collective-permute-done.14 = f32[64,3,256]{2,1,0:T(4,128)S(1)} collective-permute-done((f32[64,3,256]{2,1,0:T(4,128)S(1)}, f32[64,3,256]{2,1,0:T(4,128)S(1)}, u32[]{:S(2)}, u32[]{:S(2)}) %collective-permute-start.14) | collective-permute-done | bytes 196640 | tf_op jit(solution)/shard_map/ppermute | solution.py:19
  267.4 5.4 %fusion.3 = f32[64,16,256]{2,1,0:T(8,128)S(1)} fusion(f32[64,16,256]{2,1,0:T(8,128)S(1)} %fusion.59, f32[64,3,256]{2,1,0:T(4,128)S(1)} %collective-permute-done.15, f32[64,3,256]{2,1,0:T(4,128)S(1)} %collective-permute-done.14, f32[]{:T(128)} %bitcast.87, f32[]{:T(128)} %bitcast.86, f32[]{:T(128)} %bitcast.85, f32[]{:T(128)} %bitcast.84, f32[]{:T(128)} %bitcast.83, ...), kind=kLoop, calls=%fused_computation.227 | loop fusion | flops 4980736 | bytes 2490396 | tf_op jit(solution)/shard_map/add | solution.py:33
  272.9 6.8 %fusion.358 = f32[64,16,256]{2,1,0:T(8,128)} fusion(f32[64,16,256]{2,1,0:T(8,128)S(1)} %fusion.3, f32[]{:T(128)} %bitcast.93, f32[]{:T(128)} %bitcast.92, f32[]{:T(128)} %bitcast.91, f32[]{:T(128)} %bitcast.90, f32[]{:T(128)} %bitcast.89, f32[]{:T(128)} %bitcast.88, f32[]{:T(128)} %bitcast.1), kind=kLoop, calls=%fused_computation.582 | loop fusion | flops 3407872 | bytes 2097180 | tf_op jit(solution)/shard_map/add | solution.py:33
  279.7 22.1 %all-reduce.9.cloned.1.call-done = f32[64,16,256]{2,1,0:T(8,128)} async-done(((f32[64,16,256]{2,1,0:T(8,128)}), f32[64,16,256]{2,1,0:T(8,128)}) %all-reduce.9.cloned.1.call-update) | async-done | bytes 1048592 | tf_op jit(solution)/shard_map/psum | solution.py:57
  301.9 2.4 multiply_multiply_fusion
  (20 shorter events, 0.8 us)
Async XLA Ops:
  6.5 18.8 %copy-start = (f32[64,16,256]{2,1,0:T(8,128)S(1)}, f32[64,16,256]{2,1,0:T(8,128)}, u32[]{:S(2)}) copy-start(f32[64,16,256]{2,1,0:T(8,128)} %param.6) | copy-start | bytes 3145732
  6.5 147.6 %all-reduce.7.cloned.1.call-start = ((), (), s32[]{:S(2)}) async-start(), calls=%async_computation | async-start | bytes 2097152 | tf_op jit(solution)/shard_map/psum | solution.py:57
  7.7 17.6 %collective-permute-start = (f32[15,16,256]{2,1,0:T(8,128)S(1)}, f32[15,16,256]{2,1,0:T(8,128)S(1)}, u32[]{:S(2)}, u32[]{:S(2)}) collective-permute-start(f32[15,16,256]{2,1,0:T(8,128)S(1)} %get-tuple-element.21), channel_id=1, source_target_pairs={{0,2},{2,4},{4,6},{6,8},{8,10},{10,12},{12,14},{1,3},{3,5},{5,7},{... | collective-permute-start | bytes 737288 | tf_op jit(solution)/shard_map/ppermute | solution.py:19
  10.9 14.7 %collective-permute-start.1 = (f32[15,16,256]{2,1,0:T(8,128)S(1)}, f32[15,16,256]{2,1,0:T(8,128)S(1)}, u32[]{:S(2)}, u32[]{:S(2)}) collective-permute-start(f32[15,16,256]{2,1,0:T(8,128)S(1)} %get-tuple-element.22), channel_id=1, source_target_pairs={{2,0},{4,2},{6,4},{8,6},{10,8},{12,10},{14,12},{3,1},{5,3},{7,5},{... | collective-permute-start | bytes 737288 | tf_op jit(solution)/shard_map/ppermute | solution.py:20
  49.3 6.6 %collective-permute-start.3 = (f32[64,3,256]{2,1,0:T(4,128)S(1)}, f32[64,3,256]{2,1,0:T(4,128)S(1)}, u32[]{:S(2)}, u32[]{:S(2)}) collective-permute-start(f32[64,3,256]{2,1,0:T(4,128)S(1)} %get-tuple-element.18), channel_id=1, source_target_pairs={{1,0},{3,2},{5,4},{7,6},{9,8},{11,10},{13,12},{15,14},{17,16},{19,... | collective-permute-start | bytes 589832 | tf_op jit(solution)/shard_map/ppermute | solution.py:20
  51.5 8.2 %collective-permute-start.2 = (f32[64,3,256]{2,1,0:T(4,128)S(1)}, f32[64,3,256]{2,1,0:T(4,128)S(1)}, u32[]{:S(2)}, u32[]{:S(2)}) collective-permute-start(f32[64,3,256]{2,1,0:T(4,128)S(1)} %get-tuple-element.17), channel_id=1, source_target_pairs={{0,1},{2,3},{4,5},{6,7},{8,9},{10,11},{12,13},{14,15},{16,17},{18,... | collective-permute-start | bytes 589832 | tf_op jit(solution)/shard_map/ppermute | solution.py:19
  59.7 5.4 %copy-start.1 = (f32[1,64,16,256]{3,2,1,0:T(8,128)S(1)}, f32[1,64,16,256]{3,2,1,0:T(8,128)}, u32[]{:S(2)}) copy-start(f32[1,64,16,256]{3,2,1,0:T(8,128)} %param.5) | copy-start | bytes 3145732
  71.3 6.9 %collective-permute-start.5 = (f32[15,16,256]{2,1,0:T(8,128)S(1)}, f32[15,16,256]{2,1,0:T(8,128)S(1)}, u32[]{:S(2)}, u32[]{:S(2)}) collective-permute-start(f32[15,16,256]{2,1,0:T(8,128)S(1)} %get-tuple-element.16), channel_id=1, source_target_pairs={{2,0},{4,2},{6,4},{8,6},{10,8},{12,10},{14,12},{3,1},{5,3},{7,5},{... | collective-permute-start | bytes 737288 | tf_op jit(solution)/shard_map/ppermute | solution.py:20
  73.4 11.8 %collective-permute-start.4 = (f32[15,16,256]{2,1,0:T(8,128)S(1)}, f32[15,16,256]{2,1,0:T(8,128)S(1)}, u32[]{:S(2)}, u32[]{:S(2)}) collective-permute-start(f32[15,16,256]{2,1,0:T(8,128)S(1)} %get-tuple-element.15), channel_id=1, source_target_pairs={{0,2},{2,4},{4,6},{6,8},{8,10},{10,12},{12,14},{1,3},{3,5},{5,7},{... | collective-permute-start | bytes 737288 | tf_op jit(solution)/shard_map/ppermute | solution.py:19
  109.3 5.3 %collective-permute-start.7 = (f32[64,3,256]{2,1,0:T(4,128)S(1)}, f32[64,3,256]{2,1,0:T(4,128)S(1)}, u32[]{:S(2)}, u32[]{:S(2)}) collective-permute-start(f32[64,3,256]{2,1,0:T(4,128)S(1)} %get-tuple-element.14), channel_id=1, source_target_pairs={{1,0},{3,2},{5,4},{7,6},{9,8},{11,10},{13,12},{15,14},{17,16},{19,... | collective-permute-start | bytes 589832 | tf_op jit(solution)/shard_map/ppermute | solution.py:20
  110.6 7.8 %collective-permute-start.6 = (f32[64,3,256]{2,1,0:T(4,128)S(1)}, f32[64,3,256]{2,1,0:T(4,128)S(1)}, u32[]{:S(2)}, u32[]{:S(2)}) collective-permute-start(f32[64,3,256]{2,1,0:T(4,128)S(1)} %get-tuple-element.13), channel_id=1, source_target_pairs={{0,1},{2,3},{4,5},{6,7},{8,9},{10,11},{12,13},{14,15},{16,17},{18,... | collective-permute-start | bytes 589832 | tf_op jit(solution)/shard_map/ppermute | solution.py:19
  130.7 171.1 %all-reduce.9.cloned.1.call-start = ((), (), s32[]{:S(2)}) async-start(), calls=%async_computation.1 | async-start | bytes 2097152 | tf_op jit(solution)/shard_map/psum | solution.py:57
  155.6 14.4 %collective-permute-start.9 = (f32[15,16,256]{2,1,0:T(8,128)S(1)}, f32[15,16,256]{2,1,0:T(8,128)S(1)}, u32[]{:S(2)}, u32[]{:S(2)}) collective-permute-start(f32[15,16,256]{2,1,0:T(8,128)S(1)} %get-tuple-element.12), channel_id=1, source_target_pairs={{2,0},{4,2},{6,4},{8,6},{10,8},{12,10},{14,12},{3,1},{5,3},{7,5},{... | collective-permute-start | bytes 737288 | tf_op jit(solution)/shard_map/ppermute | solution.py:20
  158.7 11.8 %collective-permute-start.8 = (f32[15,16,256]{2,1,0:T(8,128)S(1)}, f32[15,16,256]{2,1,0:T(8,128)S(1)}, u32[]{:S(2)}, u32[]{:S(2)}) collective-permute-start(f32[15,16,256]{2,1,0:T(8,128)S(1)} %get-tuple-element.11), channel_id=1, source_target_pairs={{0,2},{2,4},{4,6},{6,8},{8,10},{10,12},{12,14},{1,3},{3,5},{5,7},{... | collective-permute-start | bytes 737288 | tf_op jit(solution)/shard_map/ppermute | solution.py:19
  194.4 7.2 %collective-permute-start.11 = (f32[64,3,256]{2,1,0:T(4,128)S(1)}, f32[64,3,256]{2,1,0:T(4,128)S(1)}, u32[]{:S(2)}, u32[]{:S(2)}) collective-permute-start(f32[64,3,256]{2,1,0:T(4,128)S(1)} %get-tuple-element.10), channel_id=1, source_target_pairs={{1,0},{3,2},{5,4},{7,6},{9,8},{11,10},{13,12},{15,14},{17,16},{19,... | collective-permute-start | bytes 589832 | tf_op jit(solution)/shard_map/ppermute | solution.py:20
  196.6 8.9 %collective-permute-start.10 = (f32[64,3,256]{2,1,0:T(4,128)S(1)}, f32[64,3,256]{2,1,0:T(4,128)S(1)}, u32[]{:S(2)}, u32[]{:S(2)}) collective-permute-start(f32[64,3,256]{2,1,0:T(4,128)S(1)} %get-tuple-element.9), channel_id=1, source_target_pairs={{0,1},{2,3},{4,5},{6,7},{8,9},{10,11},{12,13},{14,15},{16,17},{18,... | collective-permute-start | bytes 589832 | tf_op jit(solution)/shard_map/ppermute | solution.py:19
  216.9 8.9 %collective-permute-start.13 = (f32[15,16,256]{2,1,0:T(8,128)S(1)}, f32[15,16,256]{2,1,0:T(8,128)S(1)}, u32[]{:S(2)}, u32[]{:S(2)}) collective-permute-start(f32[15,16,256]{2,1,0:T(8,128)S(1)} %get-tuple-element.8), channel_id=1, source_target_pairs={{2,0},{4,2},{6,4},{8,6},{10,8},{12,10},{14,12},{3,1},{5,3},{7,5},{... | collective-permute-start | bytes 737288 | tf_op jit(solution)/shard_map/ppermute | solution.py:20
  221.2 11.8 %collective-permute-start.12 = (f32[15,16,256]{2,1,0:T(8,128)S(1)}, f32[15,16,256]{2,1,0:T(8,128)S(1)}, u32[]{:S(2)}, u32[]{:S(2)}) collective-permute-start(f32[15,16,256]{2,1,0:T(8,128)S(1)} %get-tuple-element.7), channel_id=1, source_target_pairs={{0,2},{2,4},{4,6},{6,8},{8,10},{10,12},{12,14},{1,3},{3,5},{5,7},{... | collective-permute-start | bytes 737288 | tf_op jit(solution)/shard_map/ppermute | solution.py:19
  257.0 6.6 %collective-permute-start.15 = (f32[64,3,256]{2,1,0:T(4,128)S(1)}, f32[64,3,256]{2,1,0:T(4,128)S(1)}, u32[]{:S(2)}, u32[]{:S(2)}) collective-permute-start(f32[64,3,256]{2,1,0:T(4,128)S(1)} %get-tuple-element.6), channel_id=1, source_target_pairs={{1,0},{3,2},{5,4},{7,6},{9,8},{11,10},{13,12},{15,14},{17,16},{19,... | collective-permute-start | bytes 589832 | tf_op jit(solution)/shard_map/ppermute | solution.py:20
  258.3 9.1 %collective-permute-start.14 = (f32[64,3,256]{2,1,0:T(4,128)S(1)}, f32[64,3,256]{2,1,0:T(4,128)S(1)}, u32[]{:S(2)}, u32[]{:S(2)}) collective-permute-start(f32[64,3,256]{2,1,0:T(4,128)S(1)} %get-tuple-element.5), channel_id=1, source_target_pairs={{0,1},{2,3},{4,5},{6,7},{8,9},{10,11},{12,13},{14,15},{16,17},{18,... | collective-permute-start | bytes 589832 | tf_op jit(solution)/shard_map/ppermute | solution.py:19
Sparse Core Ops, SparseCore 0:
  130.8 23.2 all-reduce.6
  279.9 21.9 all-reduce.8
where the time goes:
time: 314 us; the launch traced here: 311 us
  other arithmetic  154 us (49%)
  waiting for transfers between devices  98.3 us (31%)
  starting transfers between devices  35.3 us (11%)
  between operations  13.7 us (4%)
  local copies, waits for them, and re-layouts  9.71 us (3%)
    add x10, other arithmetic, correlate(): total + weights[offset] * lax.slice_in_dim(padded, offset, offset + lengt...  130 us
    psum x2, waiting for transfers between devices, on_device(): summed = lax.psum(correction, 'view')  45.5 us
    ppermute x8, waiting for transfers between devices, padded_2(): before = lax.ppermute(last, axis, up)  30 us
    ppermute x8, waiting for transfers between devices, padded_2(): after = lax.ppermute(first, axis, down)  22.7 us
    ppermute x8, starting transfers between devices, padded_2(): after = lax.ppermute(first, axis, down)  19.4 us
    ppermute x8, starting transfers between devices, padded_2(): before = lax.ppermute(last, axis, up)  15.8 us
    div x2, other arithmetic, on_device(): quotient = recorded / blurred  12.2 us
  transfers between devices with their start and end apart: 18, of which 16 were waited for; matrix products, arithmetic and copies ran while one was open for 5% of the time, Pallas kernels for 0%

commit v1 on v0

v1 whole, which is shorter than its diff:
```python
import functools

import jax
import jax.numpy as jnp
from jax import lax
from jax.experimental import pallas as pl
from jax.experimental.pallas import tpu as pltpu
from jax.sharding import PartitionSpec as P

ITERS = 2
MESH = pl.DeviceIdType.MESH
F32 = jnp.float32
BF16 = jnp.bfloat16


def split(x):
    high = x.astype(BF16)
    return high, (x - high.astype(F32)).astype(BF16)


def kernel(dims, obs_hbm, start_hbm, sz_ref, sy_ref, sx_ref, out_hbm,
           stage, obs_z, obs_t, mine, theirs, wf, wb, tx, zbuf, ybuf, qbuf,
           ebuf, cbuf, rybuf, rzbuf, lsem, ssem, rsem, xssem, xrsem):
    NH, NY, NX, HZ, KZ, KY, KX, S, G = dims
    my, mz, mx = KY // 2, KZ // 2, KX // 2
    NE, NR = NH + 2 * HZ, NY + 2 * my
    v = lax.axis_index("view")
    gy = lax.axis_index("gy")
    s = 2 * lax.axis_index("gz") + v
    up_z, dn_z = s < S - 1, s > 0
    up_y, dn_y = gy < G - 1, gy > 0

    def zdev(t):
        t = lax.rem(t + S, S)
        return {"view": lax.rem(t, 2), "gz": t // 2}

    def ydev(t):
        return {"gy": lax.rem(t + G, G)}

    zto = (zdev(s + 1), zdev(s - 1))
    yto = (ydev(gy + 1), ydev(gy - 1))
    partner = {"view": 1 - v}
    zhas, yhas = (up_z, dn_z), (up_y, dn_y)
    zfrom, yfrom = (dn_z, up_z), (dn_y, up_y)

    load_start = pltpu.make_async_copy(start_hbm.at[pl.ds(v * NH, NH)], stage.at[0], lsem.at[0])
    load_start.start()
    load_obs = pltpu.make_async_copy(obs_hbm.at[0, pl.ds(v * NH, NH)], obs_z.at[v], lsem.at[1])
    load_obs.start()

    barrier = pltpu.get_barrier_semaphore()
    for has, to in ((up_z, zto[0]), (dn_z, zto[1]), (up_y, yto[0]), (dn_y, yto[1])):
        @pl.when(has)
        def _(to=to):
            pl.semaphore_signal(barrier, inc=1, device_id=to, device_id_type=MESH)

    mine[...] = jnp.zeros_like(mine)
    for row, (ref, taps) in enumerate(((sz_ref, KZ), (sy_ref, KY), (sx_ref, KX))):
        raw = ref[...]
        mine[row:row + 1, 0:taps] = raw / jnp.sum(raw, axis=1, keepdims=True)
    for it in range(ITERS):
        for d in range(2):
            @pl.when(jnp.logical_not(zfrom[d]))
            def _(it=it, d=d):
                z0 = (0, HZ + NH)[d]
                ebuf[it, :, z0:z0 + HZ, :] = jnp.zeros((NR, HZ, NX), F32)

            @pl.when(jnp.logical_not(yfrom[d]))
            def _(it=it, d=d):
                r0 = (0, my + NY)[d]
                ebuf[it, r0:r0 + my] = jnp.zeros((my, NE, NX), F32)

    load_start.wait()
    ebuf[0, my:my + NY, HZ:HZ + NH, :] = jnp.transpose(stage[0], (1, 0, 2))

    peers = sum(has.astype(jnp.int32) for has in (up_z, dn_z, up_y, dn_y))
    pl.semaphore_wait(barrier, peers)

    def copy(phase, m, src, dst, to):
        return pltpu.make_async_remote_copy(
            src_ref=src, dst_ref=dst, send_sem=ssem.at[phase, m], recv_sem=rsem.at[phase, m],
            device_id=to, device_id_type=MESH)

    ROWS = ((my, my), (my + 2 * my - my, NY - 2 * my), (NY, my))
    ZED = ((HZ, NH), (0, HZ), (HZ + NH, HZ))

    def gather_z(it):
        e = ebuf.at[it]
        out = []
        for d in range(2):
            src0, dst0 = ((NH, 0), (HZ, HZ + NH))[d]
            for p, (r0, n) in enumerate(ROWS):
                out.append(copy(2 * it, 3 * d + p, e.at[pl.ds(r0, n), pl.ds(src0, HZ)],
                                e.at[pl.ds(r0, n), pl.ds(dst0, HZ)], zto[d]))
        return out

    def gather_y(it):
        e = ebuf.at[it]
        out = []
        for d in range(2):
            src0, dst0 = ((NY, 0), (my, my + NY))[d]
            for p, (z0, n) in enumerate(ZED):
                out.append(copy(2 * it, 6 + 3 * d + p, e.at[pl.ds(src0, my), pl.ds(z0, n)],
                                e.at[pl.ds(dst0, my), pl.ds(z0, n)], yto[d]))
        return out

    def when(cond, fn):
        @pl.when(cond)
        def _():
            fn()

    def both(a, b):
        return jnp.logical_and(a, b)

    zed_has = (None, dn_z, up_z)

    def gather_begin(it):
        gz_, gy_ = gather_z(it), gather_y(it)
        for p in (0, 2, 1):
            for d in range(2):
                when(zhas[d], gz_[3 * d + p].start)
        for d in range(2):
            when(yhas[d], gy_[3 * d].start)

    def gather_end(it):
        gz_, gy_ = gather_z(it), gather_y(it)
        for d in range(2):
            for p, dy in ((0, 1), (2, 0)):
                when(zfrom[d], gz_[3 * d + p].wait_recv)
                when(both(zfrom[d], yhas[dy]), gy_[3 * dy + 1 + d].start)
        for d in range(2):
            when(zfrom[d], gz_[3 * d + 1].wait_recv)
            when(yfrom[d], gy_[3 * d].wait_recv)
            for q in range(2):
                when(both(zed_has[1 + q], yfrom[d]), gy_[3 * d + 1 + q].wait_recv)
        for d in range(2):
            for p in range(3):
                when(zhas[d], gz_[3 * d + p].wait_send)
            when(yhas[d], gy_[3 * d].wait_send)
            for q in range(2):
                when(both(zed_has[1 + q], yhas[d]), gy_[3 * d + 1 + q].wait_send)

    def scatter(it):
        c, ry, rz = cbuf.at[it], rybuf.at[it], rzbuf.at[it]
        ph = 2 * it + 1
        sy_, sz_ = [], []
        for d in range(2):
            src0 = (my + NY, 0)[d]
            for p, (z0, n) in enumerate(ZED):
                sy_.append(copy(ph, 6 + 3 * d + p, c.at[pl.ds(src0, my), pl.ds(z0, n)],
                                ry.at[d, :, pl.ds(z0, n)], yto[d]))
            src0 = (HZ + NH, 0)[d]
            for p, (r0, n) in enumerate(ROWS):
                sz_.append(copy(ph, 3 * d + p, c.at[pl.ds(r0, n), pl.ds(src0, HZ)],
                                rz.at[d, pl.ds(r0 - my, n)], zto[d]))
        for q in range(2):
            for d in range(2):
                when(both(zed_has[1 + q], yhas[d]), sy_[3 * d + 1 + q].start)
        for d in range(2):
            when(zhas[d], sz_[3 * d + 1].start)
        for d in range(2):
            when(yhas[d], sy_[3 * d].start)
        for d in range(2):
            r0, piece = ((my, 0), (NY, 2))[d]
            for q in range(2):
                z0 = ZED[1 + q][0]

                def add(d=d, q=q, r0=r0, z0=z0):
                    sy_[3 * d + 1 + q].wait_recv()
                    c[r0:r0 + my, z0:z0 + HZ, :] += ry[d, :, z0:z0 + HZ, :]
                when(both(zed_has[1 + q], yfrom[d]), add)
                when(zed_has[1 + q], sz_[3 * (1 - q) + piece].start)
        for d in range(2):
            r0 = (my, NY)[d]

            def add_y(d=d, r0=r0):
                sy_[3 * d].wait_recv()
                c[r0:r0 + my, HZ:HZ + NH, :] += ry[d, :, HZ:HZ + NH, :]
            when(yfrom[d], add_y)
        for d in range(2):
            z0 = (HZ, NH)[d]

            def add_z(d=d, z0=z0):
                for p in range(3):
                    sz_[3 * d + p].wait_recv()
                c[my:my + NY, z0:z0 + HZ, :] += rz[d]
            when(zfrom[d], add_z)
        for d in range(2):
            for p in range(3):
                when(zhas[d], sz_[3 * d + p].wait_send)
            when(yhas[d], sy_[3 * d].wait_send)
            for q in range(2):
                when(both(zed_has[1 + q], yhas[d]), sy_[3 * d + 1 + q].wait_send)

    gather_begin(0)
    swap_prof = pltpu.make_async_remote_copy(
        src_ref=mine, dst_ref=theirs, send_sem=xssem.at[0], recv_sem=xrsem.at[0],
        device_id=partner, device_id_type=MESH)
    swap_prof.start()
    swap_obs = pltpu.make_async_remote_copy(
        src_ref=obs_hbm.at[0, pl.ds((1 - v) * NH, NH)], dst_ref=obs_z.at[v],
        send_sem=xssem.at[1], recv_sem=xrsem.at[1], device_id=partner, device_id_type=MESH)
    swap_obs.start()

    swap_prof.wait()
    own, other = mine[...], theirs[...]
    prof = (jnp.where(v == 0, own, other), jnp.where(v == 0, other, own))

    def tap(view, row, a):
        return prof[view][row:row + 1, a:a + 1]

    rows = lax.broadcasted_iota(jnp.int32, (NE, 3 * NE), 0)
    cols = lax.broadcasted_iota(jnp.int32, (NE, 3 * NE), 1)
    third = cols // NE
    cols = cols - third * NE

    def banded(diff, view, row, taps):
        w = jnp.zeros(diff.shape, F32)
        for a in range(taps):
            w = jnp.where(diff == a, tap(view, row, a), w)
        return w

    off = HZ - mz
    for ref, inner, outer in ((wf, rows, cols), (wb, cols, rows)):
        second = inner >= NH
        diff = outer - jnp.where(second, inner - NH, inner) - off
        w = jnp.where(second, banded(diff, 1, 0, KZ), banded(diff, 0, 0, KZ))
        high, low = split(w)
        ref[...] = jnp.where(third == 2, low.astype(F32), high.astype(F32)).astype(BF16)
    for view in range(2):
        for back in range(2):
            for r0 in range(0, NX, 64):
                r = lax.broadcasted_iota(jnp.int32, (64, NX), 0) + r0
                c = lax.broadcasted_iota(jnp.int32, (64, NX), 1)
                diff = (c - r if back else r - c) + mx
                high, low = split(banded(diff, view, 2, KX))
                tx[view, back, 0, r0:r0 + 64, :] = high
                tx[view, back, 1, r0:r0 + 64, :] = low
    wy = [[jnp.broadcast_to(tap(view, 1, b), (NH, NX)) for b in range(KY)] for view in range(2)]

    qbuf[0:2 * my] = jnp.zeros((2 * my, NE, NX), F32)
    qbuf[2 * my + NY:] = jnp.zeros((2 * my, NE, NX), F32)

    load_obs.wait()
    swap_obs.wait()
    for view in range(2):
        obs_t[view] = jnp.transpose(obs_z[view], (1, 0, 2))

    CH = 8

    def xblur(view, back):
        high, low = ybuf[0], ybuf[1]
        both_ = jnp.concatenate([high, low], axis=0)
        n = high.shape[0]
        d = jnp.dot(both_, tx[view, back, 0], preferred_element_type=F32)
        d2 = jnp.dot(high, tx[view, back, 1], preferred_element_type=F32)
        return d[:n] + (d[n:] + d2)

    def stacked(x):
        high, low = split(x)
        return jnp.concatenate([high, low, high], axis=0)

    for it in range(ITERS):
        gather_end(it)

        def zrow(y, carry):
            zbuf[y] = jnp.dot(wf[...], stacked(ebuf[it, y]), preferred_element_type=F32)
            return carry
        lax.fori_loop(0, NR, zrow, 0)

        for y0 in range(0, NY, CH):
            for view in range(2):
                z0 = view * NH
                for y in range(CH):
                    acc = wy[view][0] * zbuf[y0 + y, z0:z0 + NH, :]
                    for b in range(1, KY):
                        acc = acc + wy[view][b] * zbuf[y0 + y + b, z0:z0 + NH, :]
                    high, low = split(acc)
                    ybuf[0, y * NH:(y + 1) * NH, :] = high
                    ybuf[1, y * NH:(y + 1) * NH, :] = low
                blurred = xblur(view, 0)
                quotient = obs_t[view, y0:y0 + CH].reshape(CH * NH, NX) / blurred
                high, low = split(quotient)
                ybuf[0] = high
                ybuf[1] = low
                qbuf[2 * my + y0:2 * my + y0 + CH, z0:z0 + NH, :] = xblur(view, 1).reshape(CH, NH, NX)

        def crow(r, carry):
            parts = []
            for view in range(2):
                z0 = view * NH
                acc = wy[view][0] * qbuf[r + 2 * my, z0:z0 + NH, :]
                for b in range(1, KY):
                    acc = acc + wy[view][b] * qbuf[r + 2 * my - b, z0:z0 + NH, :]
                parts.append(acc)
            cbuf[it, r] = jnp.dot(wb[...], stacked(jnp.concatenate(parts, axis=0)),
                                  preferred_element_type=F32)
            return carry
        lax.fori_loop(0, NR, crow, 0)

        scatter(it)
        new = ebuf[it, my:my + NY, HZ:HZ + NH, :] * (0.5 * cbuf[it, my:my + NY, HZ:HZ + NH, :])
        if it + 1 < ITERS:
            ebuf[it + 1, my:my + NY, HZ:HZ + NH, :] = new
            gather_begin(it + 1)
        else:
            stage[1] = jnp.transpose(new, (1, 0, 2))
            save = pltpu.make_async_copy(stage.at[1], out_hbm.at[pl.ds(v * NH, NH)], lsem.at[2])
            save.start()
            share = pltpu.make_async_remote_copy(
                src_ref=stage.at[1], dst_ref=out_hbm.at[pl.ds(v * NH, NH)],
                send_sem=xssem.at[2], recv_sem=xrsem.at[2], device_id=partner, device_id_type=MESH)
            share.start()
            save.wait()
            share.wait()


def on_device(S, G, observed, start, spread_z, spread_y, spread_x):
    NZ, NY, NX = start.shape
    KZ, KY, KX = spread_z.shape[1], spread_y.shape[1], spread_x.shape[1]
    NH = NZ // 2
    my = KY // 2
    HZ = -(-(KZ // 2) // 8) * 8
    NE, NR = NH + 2 * HZ, NY + 2 * my
    dims = (NH, NY, NX, HZ, KZ, KY, KX, S, G)
    vm = pltpu.VMEM
    anyspec = pl.BlockSpec(memory_space=pl.ANY)
    vspec = pl.BlockSpec(memory_space=pltpu.VMEM)
    return pl.pallas_call(
        functools.partial(kernel, dims),
        out_shape=jax.ShapeDtypeStruct((NZ, NY, NX), F32),
        in_specs=[anyspec, anyspec, vspec, vspec, vspec],
        out_specs=anyspec,
        scratch_shapes=[
            vm((2, NH, NY, NX), F32), vm((2, NH, NY, NX), F32), vm((2, NY, NH, NX), F32),
            vm((8, 128), F32), vm((8, 128), F32),
            vm((NE, 3 * NE), BF16), vm((NE, 3 * NE), BF16), vm((2, 2, 2, NX, NX), BF16),
            vm((NR, NE, NX), F32), vm((2, 8 * NH, NX), BF16), vm((NY + 4 * my, NE, NX), F32),
            vm((ITERS, NR, NE, NX), F32), vm((ITERS, NR, NE, NX), F32),
            vm((ITERS, 2, my, NE, NX), F32), vm((ITERS, 2, NY, HZ, NX), F32),
            pltpu.SemaphoreType.DMA((3,)),
            pltpu.SemaphoreType.DMA((2 * ITERS, 12)), pltpu.SemaphoreType.DMA((2 * ITERS, 12)),
            pltpu.SemaphoreType.DMA((3,)), pltpu.SemaphoreType.DMA((3,)),
        ],
        compiler_params=pltpu.CompilerParams(
            collective_id=0, has_side_effects=True, vmem_limit_bytes=48 << 20),
    )(observed, start, spread_z, spread_y, spread_x)


def solution(mesh):
    S, G = 2 * mesh.shape["gz"], mesh.shape["gy"]
    return jax.shard_map(
        functools.partial(on_device, S, G),
        mesh=mesh,
        in_specs=(
            P("view", "gz", "gy", None),
            P("gz", "gy", None),
            P("view", None),
            P("view", None),
            P("view", None),
        ),
        out_specs=P("gz", "gy", None),
        check_vma=False,
    )
```

time: 314 us -> 58.1 us (0.19)
  other arithmetic: 154 us -> 0 us
  waiting for transfers between devices: 98.3 us -> 0 us
  Pallas kernels: 0 us -> 51.6 us
  starting transfers between devices: 35.3 us -> 0 us
  between operations: 13.7 us -> 0.01 us
  local copies, waits for them, and re-layouts: 9.71 us -> 5.39 us
    add x10 -> x0, other arithmetic: 130 us -> none  [correlate(): total + weights[offset] * lax.slice_in_dim(padded, offset, offset + lengt...]
    ppermute x16 -> x0, waiting for transfers between devices: 52.8 us -> none  [the longest x8 30 us: padded_2(): before = lax.ppermute(last, axis, up)]
    pallas_call x0 -> x1, Pallas kernels: none -> 51.6 us  [on_device(): pl.pallas_call(functools.partial(kernel, dims), out_shape=jax.ShapeDtypeS...]
    psum x2 -> x0, waiting for transfers between devices: 45.5 us -> none  [on_device(): summed = lax.psum(correction, 'view')]
    ppermute x16 -> x0, starting transfers between devices: 35.2 us -> none  [the longest x8 19.4 us: padded_2(): after = lax.ppermute(first, axis, down)]
    div x5 -> x0, other arithmetic: 16.1 us -> none  [the longest x2 12.2 us: on_device(): quotient = recorded / blurred]
    slice x16 -> x0, local copies, waits for them, and re-layouts: 7.17 us -> none  [the longest x6 4.12 us: correlate(): total = weights[0] * lax.slice_in_dim(padded, 0, length, 1, along)]
    unnamed x5 -> x11, local copies, waits for them, and re-layouts: 0.02 us -> 5.39 us
  transfers between devices with their start and end apart: 18 -> 0, of which waited for: 16 -> 0; matrix products, arithmetic and copies ran while one was open for 5% -> 0% of each run, Pallas kernels for 0% -> 0%
where the time goes in v1:
time: 58.1 us; the launch traced here: 57 us
  Pallas kernels  51.6 us (89%)
  local copies, waits for them, and re-layouts  5.39 us (9%)
    pallas_call x1, Pallas kernels, on_device(): pl.pallas_call(functools.partial(kernel, dims), out_shape=jax.ShapeDtypeS...  51.6 us
    unnamed x11, local copies, waits for them, and re-layouts  5.39 us

profile of v1, /device:TPU:19, one launch (start us, length us, event | category | flops | bytes accessed | tf_op | source)
XLA Modules:
  0.0 57.0 jit_solution(10705092014777990374)
XLA Ops:
  0.0 0.0 copy-start
  0.0 1.2 %copy-done = f32[1,64,16,256]{3,2,1,0:T(8,128)S(1)} copy-done((f32[1,64,16,256]{3,2,1,0:T(8,128)S(1)}, f32[1,64,16,256]{3,2,1,0:T(8,128)}, u32[]{:S(2)}) %copy-start) | copy-done | bytes 1048600
  1.2 0.0 copy-start.1
  1.2 1.2 %copy-done.1 = f32[64,16,256]{2,1,0:T(8,128)S(1)} copy-done((f32[64,16,256]{2,1,0:T(8,128)S(1)}, f32[64,16,256]{2,1,0:T(8,128)}, u32[]{:S(2)}) %copy-start.1) | copy-done | bytes 1048600
  2.5 0.0 copy-start.2
  2.5 0.7 %copy-done.2 = f32[1,31]{1,0:T(1,128)S(1)} copy-done((f32[1,31]{1,0:T(1,128)S(1)}, f32[1,31]{1,0:T(1,128)}, u32[]{:S(2)}) %copy-start.2) | copy-done | bytes 148
  3.1 0.0 copy-start.3
  3.1 0.7 %copy-done.3 = f32[1,7]{1,0:T(1,128)S(1)} copy-done((f32[1,7]{1,0:T(1,128)S(1)}, f32[1,7]{1,0:T(1,128)}, u32[]{:S(2)}) %copy-start.3) | copy-done | bytes 52
  3.8 0.0 copy-start.4
  3.8 0.7 %copy-done.4 = f32[1,7]{1,0:T(1,128)S(1)} copy-done((f32[1,7]{1,0:T(1,128)S(1)}, f32[1,7]{1,0:T(1,128)}, u32[]{:S(2)}) %copy-start.4) | copy-done | bytes 52
  4.4 51.6 %shard_map.55 = f32[64,16,256]{2,1,0:T(8,128)S(1)} custom-call(f32[1,64,16,256]{3,2,1,0:T(8,128)S(1)} %copy-done, f32[64,16,256]{2,1,0:T(8,128)S(1)} %copy-done.1, f32[1,31]{1,0:T(1,128)S(1)} %copy-done.2, f32[1,7]{1,0:T(1,128)S(1)} %copy-done.3, f32[1,7]{1,0:T(1,128)S(1)} %copy-done.4), custom_call_target="tpu_custom_call" | custom-call | tf_op jit(solution)/shard_map/pallas_call | solution.py:329
  56.0 1.0 %copy.7 = f32[64,16,256]{2,1,0:T(8,128)} copy(f32[64,16,256]{2,1,0:T(8,128)S(1)} %shard_map.55) | data formatting | bytes 2097152
Async XLA Ops:
  0.0 1.2 %copy-start = (f32[1,64,16,256]{3,2,1,0:T(8,128)S(1)}, f32[1,64,16,256]{3,2,1,0:T(8,128)}, u32[]{:S(2)}) copy-start(f32[1,64,16,256]{3,2,1,0:T(8,128)} %obs_hbm.1) | copy-start | bytes 3145732
  1.2 1.2 %copy-start.1 = (f32[64,16,256]{2,1,0:T(8,128)S(1)}, f32[64,16,256]{2,1,0:T(8,128)}, u32[]{:S(2)}) copy-start(f32[64,16,256]{2,1,0:T(8,128)} %start_hbm.1) | copy-start | bytes 3145732
  2.5 0.7 %copy-start.2 = (f32[1,31]{1,0:T(1,128)S(1)}, f32[1,31]{1,0:T(1,128)}, u32[]{:S(2)}) copy-start(f32[1,31]{1,0:T(1,128)} %sz_ref.1) | copy-start | bytes 376
  3.1 0.7 %copy-start.3 = (f32[1,7]{1,0:T(1,128)S(1)}, f32[1,7]{1,0:T(1,128)}, u32[]{:S(2)}) copy-start(f32[1,7]{1,0:T(1,128)} %sy_ref.1) | copy-start | bytes 88
  3.8 0.7 %copy-start.4 = (f32[1,7]{1,0:T(1,128)S(1)}, f32[1,7]{1,0:T(1,128)}, u32[]{:S(2)}) copy-start(f32[1,7]{1,0:T(1,128)} %sx_ref.1) | copy-start | bytes 88

commit v2 on v1

--- a/solution.py
+++ b/solution.py
@@ -19,7 +19,7 @@
 
 
 def kernel(dims, obs_hbm, start_hbm, sz_ref, sy_ref, sx_ref, out_hbm,
-           stage, obs_z, obs_t, mine, theirs, wf, wb, tx, zbuf, ybuf, qbuf,
+           raw_z, raw_y, raw_x, stage, obs_z, obs_t, mine, theirs, wf, wb, tx, zbuf, ybuf, qbuf,
            ebuf, cbuf, rybuf, rzbuf, lsem, ssem, rsem, xssem, xrsem):
     NH, NY, NX, HZ, KZ, KY, KX, S, G = dims
     my, mz, mx = KY // 2, KZ // 2, KX // 2
@@ -47,6 +47,10 @@
     load_start.start()
     load_obs = pltpu.make_async_copy(obs_hbm.at[0, pl.ds(v * NH, NH)], obs_z.at[v], lsem.at[1])
     load_obs.start()
+    loads = [pltpu.make_async_copy(ref, raw, lsem.at[3 + row])
+             for row, (ref, raw) in enumerate(((sz_ref, raw_z), (sy_ref, raw_y), (sx_ref, raw_x)))]
+    for load in loads:
+        load.start()
 
     barrier = pltpu.get_barrier_semaphore()
     for has, to in ((up_z, zto[0]), (dn_z, zto[1]), (up_y, yto[0]), (dn_y, yto[1])):
@@ -54,10 +58,6 @@
         def _(to=to):
             pl.semaphore_signal(barrier, inc=1, device_id=to, device_id_type=MESH)
 
-    mine[...] = jnp.zeros_like(mine)
-    for row, (ref, taps) in enumerate(((sz_ref, KZ), (sy_ref, KY), (sx_ref, KX))):
-        raw = ref[...]
-        mine[row:row + 1, 0:taps] = raw / jnp.sum(raw, axis=1, keepdims=True)
     for it in range(ITERS):
         for d in range(2):
             @pl.when(jnp.logical_not(zfrom[d]))
@@ -81,28 +81,10 @@
             src_ref=src, dst_ref=dst, send_sem=ssem.at[phase, m], recv_sem=rsem.at[phase, m],
             device_id=to, device_id_type=MESH)
 
-    ROWS = ((my, my), (my + 2 * my - my, NY - 2 * my), (NY, my))
+    half = (NY - 2 * my) // 2
+    ROWS = ((my, my), (NY, my), (2 * my, half), (2 * my + half, NY - 2 * my - half))
     ZED = ((HZ, NH), (0, HZ), (HZ + NH, HZ))
-
-    def gather_z(it):
-        e = ebuf.at[it]
-        out = []
-        for d in range(2):
-            src0, dst0 = ((NH, 0), (HZ, HZ + NH))[d]
-            for p, (r0, n) in enumerate(ROWS):
-                out.append(copy(2 * it, 3 * d + p, e.at[pl.ds(r0, n), pl.ds(src0, HZ)],
-                                e.at[pl.ds(r0, n), pl.ds(dst0, HZ)], zto[d]))
-        return out
-
-    def gather_y(it):
-        e = ebuf.at[it]
-        out = []
-        for d in range(2):
-            src0, dst0 = ((NY, 0), (my, my + NY))[d]
-            for p, (z0, n) in enumerate(ZED):
-                out.append(copy(2 * it, 6 + 3 * d + p, e.at[pl.ds(src0, my), pl.ds(z0, n)],
-                                e.at[pl.ds(dst0, my), pl.ds(z0, n)], yto[d]))
-        return out
+    ENDS, MID = (0, 1), (2, 3)
 
     def when(cond, fn):
         @pl.when(cond)
@@ -114,85 +96,104 @@
 
     zed_has = (None, dn_z, up_z)
 
-    def gather_begin(it):
-        gz_, gy_ = gather_z(it), gather_y(it)
-        for p in (0, 2, 1):
-            for d in range(2):
-                when(zhas[d], gz_[3 * d + p].start)
-        for d in range(2):
-            when(yhas[d], gy_[3 * d].start)
-
-    def gather_end(it):
-        gz_, gy_ = gather_z(it), gather_y(it)
-        for d in range(2):
-            for p, dy in ((0, 1), (2, 0)):
-                when(zfrom[d], gz_[3 * d + p].wait_recv)
-                when(both(zfrom[d], yhas[dy]), gy_[3 * dy + 1 + d].start)
-        for d in range(2):
-            when(zfrom[d], gz_[3 * d + 1].wait_recv)
-            when(yfrom[d], gy_[3 * d].wait_recv)
+    def gz(it, d, p):
+        e = ebuf.at[it]
+        src0, dst0 = ((NH, 0), (HZ, HZ + NH))[d]
+        r0, n = ROWS[p]
+        return copy(2 * it, 4 * d + p, e.at[pl.ds(r0, n), pl.ds(src0, HZ)],
+                    e.at[pl.ds(r0, n), pl.ds(dst0, HZ)], zto[d])
+
+    def gyc(it, d, p):
+        e = ebuf.at[it]
+        src0, dst0 = ((NY, 0), (my, my + NY))[d]
+        z0, n = ZED[p]
+        return copy(2 * it, 8 + 3 * d + p, e.at[pl.ds(src0, my), pl.ds(z0, n)],
+                    e.at[pl.ds(dst0, my), pl.ds(z0, n)], yto[d])
+
+    def sz(it, d, p):
+        src0 = (HZ + NH, 0)[d]
+        r0, n = ROWS[p]
+        return copy(2 * it + 1, 4 * d + p, cbuf.at[it, pl.ds(r0, n), pl.ds(src0, HZ)],
+                    rzbuf.at[it, d, pl.ds(r0 - my, n)], zto[d])
+
+    def sy(it, d, p):
+        src0 = (my + NY, 0)[d]
+        z0, n = ZED[p]
+        return copy(2 * it + 1, 8 + 3 * d + p, cbuf.at[it, pl.ds(src0, my), pl.ds(z0, n)],
+                    rybuf.at[it, d, :, pl.ds(z0, n)], yto[d])
+
+    def gather_piece(it, p):
+        for d in range(2):
+            when(zhas[d], gz(it, d, p).start)
+
+    def gather_own(it):
+        for d in range(2):
+            when(yhas[d], gyc(it, d, 0).start)
+
+    def gather_take(it, p):
+        for d in range(2):
+            when(zfrom[d], gz(it, d, p).wait_recv)
+            if p in ENDS:
+                dy = 1 - p
+                when(both(zfrom[d], yhas[dy]), gyc(it, dy, 1 + d).start)
+
+    def gather_edge(it, d):
+        when(yfrom[d], gyc(it, d, 0).wait_recv)
+        for q in range(2):
+            when(both(zed_has[1 + q], yfrom[d]), gyc(it, d, 1 + q).wait_recv)
+
+    def sent(it, z, y):
+        for d in range(2):
+            for p in range(4):
+                when(zhas[d], z(it, d, p).wait_send)
+            when(yhas[d], y(it, d, 0).wait_send)
             for q in range(2):
-                when(both(zed_has[1 + q], yfrom[d]), gy_[3 * d + 1 + q].wait_recv)
-        for d in range(2):
-            for p in range(3):
-                when(zhas[d], gz_[3 * d + p].wait_send)
-            when(yhas[d], gy_[3 * d].wait_send)
-            for q in range(2):
-                when(both(zed_has[1 + q], yhas[d]), gy_[3 * d + 1 + q].wait_send)
-
-    def scatter(it):
-        c, ry, rz = cbuf.at[it], rybuf.at[it], rzbuf.at[it]
-        ph = 2 * it + 1
-        sy_, sz_ = [], []
-        for d in range(2):
-            src0 = (my + NY, 0)[d]
-            for p, (z0, n) in enumerate(ZED):
-                sy_.append(copy(ph, 6 + 3 * d + p, c.at[pl.ds(src0, my), pl.ds(z0, n)],
-                                ry.at[d, :, pl.ds(z0, n)], yto[d]))
-            src0 = (HZ + NH, 0)[d]
-            for p, (r0, n) in enumerate(ROWS):
-                sz_.append(copy(ph, 3 * d + p, c.at[pl.ds(r0, n), pl.ds(src0, HZ)],
-                                rz.at[d, pl.ds(r0 - my, n)], zto[d]))
+                when(both(zed_has[1 + q], yhas[d]), y(it, d, 1 + q).wait_send)
+
+    def scatter_edges(it):
         for q in range(2):
             for d in range(2):
-                when(both(zed_has[1 + q], yhas[d]), sy_[3 * d + 1 + q].start)
-        for d in range(2):
-            when(zhas[d], sz_[3 * d + 1].start)
-        for d in range(2):
-            when(yhas[d], sy_[3 * d].start)
-        for d in range(2):
-            r0, piece = ((my, 0), (NY, 2))[d]
-            for q in range(2):
-                z0 = ZED[1 + q][0]
-
-                def add(d=d, q=q, r0=r0, z0=z0):
-                    sy_[3 * d + 1 + q].wait_recv()
-                    c[r0:r0 + my, z0:z0 + HZ, :] += ry[d, :, z0:z0 + HZ, :]
-                when(both(zed_has[1 + q], yfrom[d]), add)
-                when(zed_has[1 + q], sz_[3 * (1 - q) + piece].start)
-        for d in range(2):
-            r0 = (my, NY)[d]
-
-            def add_y(d=d, r0=r0):
-                sy_[3 * d].wait_recv()
-                c[r0:r0 + my, HZ:HZ + NH, :] += ry[d, :, HZ:HZ + NH, :]
-            when(yfrom[d], add_y)
+                when(both(zed_has[1 + q], yhas[d]), sy(it, d, 1 + q).start)
+        for d in range(2):
+            when(yhas[d], sy(it, d, 0).start)
+
+    def scatter_piece(it, p):
+        for d in range(2):
+            when(zhas[d], sz(it, d, p).start)
+
+    def scatter_end(it, p):
+        d, r0 = p, ROWS[p][0]
+        for q in range(2):
+            z0 = ZED[1 + q][0]
+
+            def add(q=q, z0=z0):
+                sy(it, d, 1 + q).wait_recv()
+                cbuf[it, r0:r0 + my, z0:z0 + HZ, :] += rybuf[it, d, :, z0:z0 + HZ, :]
+            when(both(zed_has[1 + q], yfrom[d]), add)
+            when(zed_has[1 + q], sz(it, 1 - q, p).start)
+
+    def scatter_take(it, p):
+        r0, n = ROWS[p]
+        if p in ENDS:
+            def add_y():
+                sy(it, p, 0).wait_recv()
+                cbuf[it, r0:r0 + n, HZ:HZ + NH, :] += rybuf[it, p, :, HZ:HZ + NH, :]
+            when(yfrom[p], add_y)
         for d in range(2):
             z0 = (HZ, NH)[d]
 
             def add_z(d=d, z0=z0):
-                for p in range(3):
-                    sz_[3 * d + p].wait_recv()
-                c[my:my + NY, z0:z0 + HZ, :] += rz[d]
+                sz(it, d, p).wait_recv()
+                cbuf[it, r0:r0 + n, z0:z0 + HZ, :] += rzbuf[it, d, r0 - my:r0 - my + n]
             when(zfrom[d], add_z)
-        for d in range(2):
-            for p in range(3):
-                when(zhas[d], sz_[3 * d + p].wait_send)
-            when(yhas[d], sy_[3 * d].wait_send)
-            for q in range(2):
-                when(both(zed_has[1 + q], yhas[d]), sy_[3 * d + 1 + q].wait_send)
-
-    gather_begin(0)
+
+    for p in (0, 1, 2, 3):
+        gather_piece(0, p)
+    gather_own(0)
+    mine[...] = jnp.zeros_like(mine)
+    for row, (raw, taps) in enumerate(((raw_z, KZ), (raw_y, KY), (raw_x, KX))):
+        loads[row].wait()
+        mine[row:row + 1, 0:taps] = raw[...] / jnp.sum(raw[...], axis=1, keepdims=True)
     swap_prof = pltpu.make_async_remote_copy(
         src_ref=mine, dst_ref=theirs, send_sem=xssem.at[0], recv_sem=xrsem.at[0],
         device_id=partner, device_id_type=MESH)
@@ -261,12 +262,19 @@
         return jnp.concatenate([high, low, high], axis=0)
 
     for it in range(ITERS):
-        gather_end(it)
-
-        def zrow(y, carry):
+        def zrow(y, carry, it=it):
             zbuf[y] = jnp.dot(wf[...], stacked(ebuf[it, y]), preferred_element_type=F32)
             return carry
-        lax.fori_loop(0, NR, zrow, 0)
+
+        def zrows(r0, n):
+            lax.fori_loop(r0, r0 + n, zrow, 0, unroll=True)
+
+        for p in ((0, 1, 2, 3) if it == 0 else (2, 0, 1, 3)):
+            gather_take(it, p)
+            zrows(*ROWS[p])
+        for d in range(2):
+            gather_edge(it, d)
+            zrows((0, my + NY)[d], my)
 
         for y0 in range(0, NY, CH):
             for view in range(2):
@@ -285,7 +293,7 @@
                 ybuf[1] = low
                 qbuf[2 * my + y0:2 * my + y0 + CH, z0:z0 + NH, :] = xblur(view, 1).reshape(CH, NH, NX)
 
-        def crow(r, carry):
+        def crow(r, carry, it=it):
             parts = []
             for view in range(2):
                 z0 = view * NH
@@ -296,15 +304,43 @@
             cbuf[it, r] = jnp.dot(wb[...], stacked(jnp.concatenate(parts, axis=0)),
                                   preferred_element_type=F32)
             return carry
-        lax.fori_loop(0, NR, crow, 0)
-
-        scatter(it)
-        new = ebuf[it, my:my + NY, HZ:HZ + NH, :] * (0.5 * cbuf[it, my:my + NY, HZ:HZ + NH, :])
+        def crows(r0, n):
+            lax.fori_loop(r0, r0 + n, crow, 0, unroll=True)
+
+        crows(0, my)
+        crows(my + NY, my)
+        scatter_edges(it)
+        for p in MID:
+            crows(*ROWS[p])
+            scatter_piece(it, p)
+        for p in ENDS:
+            crows(*ROWS[p])
+        for p in ENDS:
+            scatter_end(it, p)
+
+        def update(p, it=it):
+            r0, n = ROWS[p]
+            scatter_take(it, p)
+            new = ebuf[it, r0:r0 + n, HZ:HZ + NH, :] * (0.5 * cbuf[it, r0:r0 + n, HZ:HZ + NH, :])
+            if it + 1 < ITERS:
+                ebuf[it + 1, r0:r0 + n, HZ:HZ + NH, :] = new
+            else:
+                zbuf[r0:r0 + n, 0:NH, :] = new
+
         if it + 1 < ITERS:
-            ebuf[it + 1, my:my + NY, HZ:HZ + NH, :] = new
-            gather_begin(it + 1)
+            update(2)
+            gather_piece(it + 1, 2)
+            update(3)
+            update(0)
+            gather_piece(it + 1, 0)
+            update(1)
+            gather_piece(it + 1, 1)
+            gather_own(it + 1)
+            gather_piece(it + 1, 3)
         else:
-            stage[1] = jnp.transpose(new, (1, 0, 2))
+            for p in (2, 3, 0, 1):
+                update(p)
+            stage[1] = jnp.transpose(zbuf[my:my + NY, 0:NH, :], (1, 0, 2))
             save = pltpu.make_async_copy(stage.at[1], out_hbm.at[pl.ds(v * NH, NH)], lsem.at[2])
             save.start()
             share = pltpu.make_async_remote_copy(
@@ -313,6 +349,9 @@
             share.start()
             save.wait()
             share.wait()
+    for it in range(ITERS):
+        sent(it, gz, gyc)
+        sent(it, sz, sy)
 
 
 def on_device(S, G, observed, start, spread_z, spread_y, spread_x):
@@ -324,22 +363,22 @@
     NE, NR = NH + 2 * HZ, NY + 2 * my
     dims = (NH, NY, NX, HZ, KZ, KY, KX, S, G)
     vm = pltpu.VMEM
-    anyspec = pl.BlockSpec(memory_space=pl.ANY)
-    vspec = pl.BlockSpec(memory_space=pltpu.VMEM)
+    hbm = pl.BlockSpec(memory_space=pltpu.HBM)
     return pl.pallas_call(
         functools.partial(kernel, dims),
         out_shape=jax.ShapeDtypeStruct((NZ, NY, NX), F32),
-        in_specs=[anyspec, anyspec, vspec, vspec, vspec],
-        out_specs=anyspec,
+        in_specs=[hbm] * 5,
+        out_specs=hbm,
         scratch_shapes=[
+            vm((1, KZ), F32), vm((1, KY), F32), vm((1, KX), F32),
             vm((2, NH, NY, NX), F32), vm((2, NH, NY, NX), F32), vm((2, NY, NH, NX), F32),
             vm((8, 128), F32), vm((8, 128), F32),
             vm((NE, 3 * NE), BF16), vm((NE, 3 * NE), BF16), vm((2, 2, 2, NX, NX), BF16),
             vm((NR, NE, NX), F32), vm((2, 8 * NH, NX), BF16), vm((NY + 4 * my, NE, NX), F32),
             vm((ITERS, NR, NE, NX), F32), vm((ITERS, NR, NE, NX), F32),
             vm((ITERS, 2, my, NE, NX), F32), vm((ITERS, 2, NY, HZ, NX), F32),
-            pltpu.SemaphoreType.DMA((3,)),
-            pltpu.SemaphoreType.DMA((2 * ITERS, 12)), pltpu.SemaphoreType.DMA((2 * ITERS, 12)),
+            pltpu.SemaphoreType.DMA((6,)),
+            pltpu.SemaphoreType.DMA((2 * ITERS, 14)), pltpu.SemaphoreType.DMA((2 * ITERS, 14)),
             pltpu.SemaphoreType.DMA((3,)), pltpu.SemaphoreType.DMA((3,)),
         ],
         compiler_params=pltpu.CompilerParams(

time: 58.1 us -> 45.2 us (0.78)
  the two profiles are of different devices: /device:TPU:19 before, /device:TPU:27 now
where the time goes in v2:
time: 45.2 us; the launch traced here: 44.9 us
  Pallas kernels  39.5 us (87%)
  local copies, waits for them, and re-layouts  5.39 us (12%)
    pallas_call x1, Pallas kernels, on_device(): pl.pallas_call(functools.partial(kernel, dims), out_shape=jax.ShapeDtypeS...  39.5 us
    unnamed x11, local copies, waits for them, and re-layouts  5.39 us

profile of v2, /device:TPU:27, one launch (start us, length us, event | category | flops | bytes accessed | tf_op | source)
XLA Modules:
  0.0 44.9 jit_solution(12948144455879938209)
XLA Ops:
  0.0 0.0 copy-start
  0.0 1.2 %copy-done = f32[1,64,16,256]{3,2,1,0:T(8,128)S(1)} copy-done((f32[1,64,16,256]{3,2,1,0:T(8,128)S(1)}, f32[1,64,16,256]{3,2,1,0:T(8,128)}, u32[]{:S(2)}) %copy-start) | copy-done | bytes 1048600
  1.2 0.0 copy-start.1
  1.2 1.2 %copy-done.1 = f32[64,16,256]{2,1,0:T(8,128)S(1)} copy-done((f32[64,16,256]{2,1,0:T(8,128)S(1)}, f32[64,16,256]{2,1,0:T(8,128)}, u32[]{:S(2)}) %copy-start.1) | copy-done | bytes 1048600
  2.5 0.0 copy-start.2
  2.5 0.7 %copy-done.2 = f32[1,31]{1,0:T(1,128)S(1)} copy-done((f32[1,31]{1,0:T(1,128)S(1)}, f32[1,31]{1,0:T(1,128)}, u32[]{:S(2)}) %copy-start.2) | copy-done | bytes 148
  3.1 0.0 copy-start.3
  3.1 0.7 %copy-done.3 = f32[1,7]{1,0:T(1,128)S(1)} copy-done((f32[1,7]{1,0:T(1,128)S(1)}, f32[1,7]{1,0:T(1,128)}, u32[]{:S(2)}) %copy-start.3) | copy-done | bytes 52
  3.8 0.0 copy-start.4
  3.8 0.7 %copy-done.4 = f32[1,7]{1,0:T(1,128)S(1)} copy-done((f32[1,7]{1,0:T(1,128)S(1)}, f32[1,7]{1,0:T(1,128)}, u32[]{:S(2)}) %copy-start.4) | copy-done | bytes 52
  4.4 39.5 %shard_map.55 = f32[64,16,256]{2,1,0:T(8,128)S(1)} custom-call(f32[1,64,16,256]{3,2,1,0:T(8,128)S(1)} %copy-done, f32[64,16,256]{2,1,0:T(8,128)S(1)} %copy-done.1, f32[1,31]{1,0:T(1,128)S(1)} %copy-done.2, f32[1,7]{1,0:T(1,128)S(1)} %copy-done.3, f32[1,7]{1,0:T(1,128)S(1)} %copy-done.4), custom_call_target="tpu_custom_call" | custom-call | tf_op jit(solution)/shard_map/pallas_call | solution.py:367
  44.0 1.0 %copy.7 = f32[64,16,256]{2,1,0:T(8,128)} copy(f32[64,16,256]{2,1,0:T(8,128)S(1)} %shard_map.55) | data formatting | bytes 2097152
Async XLA Ops:
  0.0 1.2 %copy-start = (f32[1,64,16,256]{3,2,1,0:T(8,128)S(1)}, f32[1,64,16,256]{3,2,1,0:T(8,128)}, u32[]{:S(2)}) copy-start(f32[1,64,16,256]{3,2,1,0:T(8,128)} %obs_hbm.1) | copy-start | bytes 3145732
  1.2 1.2 %copy-start.1 = (f32[64,16,256]{2,1,0:T(8,128)S(1)}, f32[64,16,256]{2,1,0:T(8,128)}, u32[]{:S(2)}) copy-start(f32[64,16,256]{2,1,0:T(8,128)} %start_hbm.1) | copy-start | bytes 3145732
  2.5 0.7 %copy-start.2 = (f32[1,31]{1,0:T(1,128)S(1)}, f32[1,31]{1,0:T(1,128)}, u32[]{:S(2)}) copy-start(f32[1,31]{1,0:T(1,128)} %sz_ref.1) | copy-start | bytes 376
  3.1 0.7 %copy-start.3 = (f32[1,7]{1,0:T(1,128)S(1)}, f32[1,7]{1,0:T(1,128)}, u32[]{:S(2)}) copy-start(f32[1,7]{1,0:T(1,128)} %sy_ref.1) | copy-start | bytes 88
  3.8 0.7 %copy-start.4 = (f32[1,7]{1,0:T(1,128)S(1)}, f32[1,7]{1,0:T(1,128)}, u32[]{:S(2)}) copy-start(f32[1,7]{1,0:T(1,128)} %sx_ref.1) | copy-start | bytes 88

commit v3 on v2

--- a/solution.py
+++ b/solution.py
@@ -20,7 +20,7 @@
 
 def kernel(dims, obs_hbm, start_hbm, sz_ref, sy_ref, sx_ref, out_hbm,
            raw_z, raw_y, raw_x, stage, obs_z, obs_t, mine, theirs, wf, wb, tx, zbuf, ybuf, qbuf,
-           ebuf, cbuf, rybuf, rzbuf, lsem, ssem, rsem, xssem, xrsem):
+           ebuf, cbuf, rybuf, rzbuf, lsem, osem, ssem, rsem, xssem, xrsem):
     NH, NY, NX, HZ, KZ, KY, KX, S, G = dims
     my, mz, mx = KY // 2, KZ // 2, KX // 2
     NE, NR = NH + 2 * HZ, NY + 2 * my
@@ -81,10 +81,11 @@
             src_ref=src, dst_ref=dst, send_sem=ssem.at[phase, m], recv_sem=rsem.at[phase, m],
             device_id=to, device_id_type=MESH)
 
-    half = (NY - 2 * my) // 2
-    ROWS = ((my, my), (NY, my), (2 * my, half), (2 * my + half, NY - 2 * my - half))
+    CH = NY // 2
+    ROWS = ((my, my), (NY, my), (2 * my, CH - 2 * my), (CH, 2 * my), (CH + 2 * my, NY - CH - 2 * my))
+    NP = len(ROWS)
     ZED = ((HZ, NH), (0, HZ), (HZ + NH, HZ))
-    ENDS, MID = (0, 1), (2, 3)
+    ENDS = (0, 1)
 
     def when(cond, fn):
         @pl.when(cond)
@@ -100,26 +101,26 @@
         e = ebuf.at[it]
         src0, dst0 = ((NH, 0), (HZ, HZ + NH))[d]
         r0, n = ROWS[p]
-        return copy(2 * it, 4 * d + p, e.at[pl.ds(r0, n), pl.ds(src0, HZ)],
+        return copy(2 * it, NP * d + p, e.at[pl.ds(r0, n), pl.ds(src0, HZ)],
                     e.at[pl.ds(r0, n), pl.ds(dst0, HZ)], zto[d])
 
     def gyc(it, d, p):
         e = ebuf.at[it]
         src0, dst0 = ((NY, 0), (my, my + NY))[d]
         z0, n = ZED[p]
-        return copy(2 * it, 8 + 3 * d + p, e.at[pl.ds(src0, my), pl.ds(z0, n)],
+        return copy(2 * it, 2 * NP + 3 * d + p, e.at[pl.ds(src0, my), pl.ds(z0, n)],
                     e.at[pl.ds(dst0, my), pl.ds(z0, n)], yto[d])
 
     def sz(it, d, p):
         src0 = (HZ + NH, 0)[d]
         r0, n = ROWS[p]
-        return copy(2 * it + 1, 4 * d + p, cbuf.at[it, pl.ds(r0, n), pl.ds(src0, HZ)],
+        return copy(2 * it + 1, NP * d + p, cbuf.at[it, pl.ds(r0, n), pl.ds(src0, HZ)],
                     rzbuf.at[it, d, pl.ds(r0 - my, n)], zto[d])
 
     def sy(it, d, p):
         src0 = (my + NY, 0)[d]
         z0, n = ZED[p]
-        return copy(2 * it + 1, 8 + 3 * d + p, cbuf.at[it, pl.ds(src0, my), pl.ds(z0, n)],
+        return copy(2 * it + 1, 2 * NP + 3 * d + p, cbuf.at[it, pl.ds(src0, my), pl.ds(z0, n)],
                     rybuf.at[it, d, :, pl.ds(z0, n)], yto[d])
 
     def gather_piece(it, p):
@@ -144,18 +145,16 @@
 
     def sent(it, z, y):
         for d in range(2):
-            for p in range(4):
+            for p in range(NP):
                 when(zhas[d], z(it, d, p).wait_send)
             when(yhas[d], y(it, d, 0).wait_send)
             for q in range(2):
                 when(both(zed_has[1 + q], yhas[d]), y(it, d, 1 + q).wait_send)
 
-    def scatter_edges(it):
+    def scatter_edge(it, d):
         for q in range(2):
-            for d in range(2):
-                when(both(zed_has[1 + q], yhas[d]), sy(it, d, 1 + q).start)
-        for d in range(2):
-            when(yhas[d], sy(it, d, 0).start)
+            when(both(zed_has[1 + q], yhas[d]), sy(it, d, 1 + q).start)
+        when(yhas[d], sy(it, d, 0).start)
 
     def scatter_piece(it, p):
         for d in range(2):
@@ -187,7 +186,7 @@
                 cbuf[it, r0:r0 + n, z0:z0 + HZ, :] += rzbuf[it, d, r0 - my:r0 - my + n]
             when(zfrom[d], add_z)
 
-    for p in (0, 1, 2, 3):
+    for p in range(NP):
         gather_piece(0, p)
     gather_own(0)
     mine[...] = jnp.zeros_like(mine)
@@ -247,8 +246,6 @@
     for view in range(2):
         obs_t[view] = jnp.transpose(obs_z[view], (1, 0, 2))
 
-    CH = 8
-
     def xblur(view, back):
         high, low = ybuf[0], ybuf[1]
         both_ = jnp.concatenate([high, low], axis=0)
@@ -269,14 +266,7 @@
         def zrows(r0, n):
             lax.fori_loop(r0, r0 + n, zrow, 0, unroll=True)
 
-        for p in ((0, 1, 2, 3) if it == 0 else (2, 0, 1, 3)):
-            gather_take(it, p)
-            zrows(*ROWS[p])
-        for d in range(2):
-            gather_edge(it, d)
-            zrows((0, my + NY)[d], my)
-
-        for y0 in range(0, NY, CH):
+        def half(y0, it=it):
             for view in range(2):
                 z0 = view * NH
                 for y in range(CH):
@@ -307,15 +297,28 @@
         def crows(r0, n):
             lax.fori_loop(r0, r0 + n, crow, 0, unroll=True)
 
+        for p in ((0, 1, 2, 3) if it == 0 else (2, 0, 1, 3)):
+            gather_take(it, p)
+            zrows(*ROWS[p])
+        gather_edge(it, 0)
+        zrows(0, my)
+        half(0)
         crows(0, my)
+        scatter_edge(it, 1)
+        crows(*ROWS[2])
+        scatter_piece(it, 2)
+        gather_take(it, 4)
+        zrows(*ROWS[4])
+        gather_edge(it, 1)
+        zrows(my + NY, my)
+        half(CH)
         crows(my + NY, my)
-        scatter_edges(it)
-        for p in MID:
+        scatter_edge(it, 0)
+        for p in (3, 4):
             crows(*ROWS[p])
             scatter_piece(it, p)
         for p in ENDS:
             crows(*ROWS[p])
-        for p in ENDS:
             scatter_end(it, p)
 
         def update(p, it=it):
@@ -331,24 +334,29 @@
             update(2)
             gather_piece(it + 1, 2)
             update(3)
+            update(4)
             update(0)
             gather_piece(it + 1, 0)
             update(1)
             gather_piece(it + 1, 1)
             gather_own(it + 1)
             gather_piece(it + 1, 3)
+            gather_piece(it + 1, 4)
         else:
-            for p in (2, 3, 0, 1):
+            outs = []
+            for n, p in enumerate((2, 3, 4, 0, 1)):
                 update(p)
-            stage[1] = jnp.transpose(zbuf[my:my + NY, 0:NH, :], (1, 0, 2))
-            save = pltpu.make_async_copy(stage.at[1], out_hbm.at[pl.ds(v * NH, NH)], lsem.at[2])
-            save.start()
-            share = pltpu.make_async_remote_copy(
-                src_ref=stage.at[1], dst_ref=out_hbm.at[pl.ds(v * NH, NH)],
-                send_sem=xssem.at[2], recv_sem=xrsem.at[2], device_id=partner, device_id_type=MESH)
-            share.start()
-            save.wait()
-            share.wait()
+                r0, rows_ = ROWS[p]
+                src = zbuf.at[pl.ds(r0, rows_), pl.ds(0, NH)]
+                dst = out_hbm.at[pl.ds(r0 - my, rows_), pl.ds(v * NH, NH)]
+                outs.append(pltpu.make_async_copy(src, dst, osem.at[n]))
+                outs.append(pltpu.make_async_remote_copy(
+                    src_ref=src, dst_ref=dst, send_sem=xssem.at[2 + n], recv_sem=xrsem.at[2 + n],
+                    device_id=partner, device_id_type=MESH))
+                outs[-1].start()
+                outs[-2].start()
+            for out in outs:
+                out.wait()
     for it in range(ITERS):
         sent(it, gz, gyc)
         sent(it, sz, sy)
@@ -364,26 +372,27 @@
     dims = (NH, NY, NX, HZ, KZ, KY, KX, S, G)
     vm = pltpu.VMEM
     hbm = pl.BlockSpec(memory_space=pltpu.HBM)
-    return pl.pallas_call(
+    out = pl.pallas_call(
         functools.partial(kernel, dims),
-        out_shape=jax.ShapeDtypeStruct((NZ, NY, NX), F32),
+        out_shape=jax.ShapeDtypeStruct((NY, NZ, NX), F32),
         in_specs=[hbm] * 5,
         out_specs=hbm,
         scratch_shapes=[
             vm((1, KZ), F32), vm((1, KY), F32), vm((1, KX), F32),
-            vm((2, NH, NY, NX), F32), vm((2, NH, NY, NX), F32), vm((2, NY, NH, NX), F32),
+            vm((1, NH, NY, NX), F32), vm((2, NH, NY, NX), F32), vm((2, NY, NH, NX), F32),
             vm((8, 128), F32), vm((8, 128), F32),
             vm((NE, 3 * NE), BF16), vm((NE, 3 * NE), BF16), vm((2, 2, 2, NX, NX), BF16),
-            vm((NR, NE, NX), F32), vm((2, 8 * NH, NX), BF16), vm((NY + 4 * my, NE, NX), F32),
+            vm((NR, NE, NX), F32), vm((2, NY // 2 * NH, NX), BF16), vm((NY + 4 * my, NE, NX), F32),
             vm((ITERS, NR, NE, NX), F32), vm((ITERS, NR, NE, NX), F32),
             vm((ITERS, 2, my, NE, NX), F32), vm((ITERS, 2, NY, HZ, NX), F32),
-            pltpu.SemaphoreType.DMA((6,)),
-            pltpu.SemaphoreType.DMA((2 * ITERS, 14)), pltpu.SemaphoreType.DMA((2 * ITERS, 14)),
-            pltpu.SemaphoreType.DMA((3,)), pltpu.SemaphoreType.DMA((3,)),
+            pltpu.SemaphoreType.DMA((6,)), pltpu.SemaphoreType.DMA((5,)),
+            pltpu.SemaphoreType.DMA((2 * ITERS, 16)), pltpu.SemaphoreType.DMA((2 * ITERS, 16)),
+            pltpu.SemaphoreType.DMA((7,)), pltpu.SemaphoreType.DMA((7,)),
         ],
         compiler_params=pltpu.CompilerParams(
-            collective_id=0, has_side_effects=True, vmem_limit_bytes=48 << 20),
+            collective_id=0, has_side_effects=True, vmem_limit_bytes=67043328),
     )(observed, start, spread_z, spread_y, spread_x)
+    return jnp.transpose(out, (1, 0, 2))
 
 
 def solution(mesh):

time: 45.2 us -> 41.1 us (0.909)
  the two profiles are of different devices: /device:TPU:27 before, /device:TPU:19 now
where the time goes in v3:
time: 41.1 us; the launch traced here: 41 us
  Pallas kernels  38.2 us (93%)
  local copies, waits for them, and re-layouts  2.81 us (7%)
    pallas_call x1, Pallas kernels, on_device(): pl.pallas_call(functools.partial(kernel, dims), out_shape=jax.ShapeDtypeS...  38.2 us
    transpose x1, local copies, waits for them, and re-layouts, on_device(): return jnp.transpose(out, (1, 0, 2))  2.81 us

profile of v3, /device:TPU:19, one launch (start us, length us, event | category | flops | bytes accessed | tf_op | source)
XLA Modules:
  0.0 41.0 jit_solution(10493885689295133723)
XLA Ops:
  0.0 38.2 %shard_map.55 = f32[16,64,256]{2,1,0:T(8,128)} custom-call(f32[1,64,16,256]{3,2,1,0:T(8,128)} %obs_hbm.1, f32[64,16,256]{2,1,0:T(8,128)} %start_hbm.1, f32[1,31]{1,0:T(1,128)} %sz_ref.1, f32[1,7]{1,0:T(1,128)} %sy_ref.1, f32[1,7]{1,0:T(1,128)} %sx_ref.1), custom_call_target="tpu_custom_call" | custom-call | tf_op jit(solution)/shard_map/pallas_call | solution.py:375
  38.2 2.8 %copy.6 = f32[64,16,256]{2,1,0:T(8,128)} copy(f32[64,16,256]{2,0,1:T(8,128)} %bitcast.1) | data formatting | bytes 2097152 | tf_op jit(solution)/shard_map/transpose | solution.py:395

commit v4 on v3

--- a/solution.py
+++ b/solution.py
@@ -362,6 +362,10 @@
         sent(it, sz, sy)
 
 
+def turn(x_ref, o_ref):
+    o_ref[...] = jnp.transpose(x_ref[...], (1, 0, 2))
+
+
 def on_device(S, G, observed, start, spread_z, spread_y, spread_x):
     NZ, NY, NX = start.shape
     KZ, KY, KX = spread_z.shape[1], spread_y.shape[1], spread_x.shape[1]
@@ -392,7 +396,14 @@
         compiler_params=pltpu.CompilerParams(
             collective_id=0, has_side_effects=True, vmem_limit_bytes=67043328),
     )(observed, start, spread_z, spread_y, spread_x)
-    return jnp.transpose(out, (1, 0, 2))
+    block = NZ // 4
+    return pl.pallas_call(
+        turn,
+        grid=(NZ // block,),
+        out_shape=jax.ShapeDtypeStruct((NZ, NY, NX), F32),
+        in_specs=[pl.BlockSpec((NY, block, NX), lambda i: (0, i, 0))],
+        out_specs=pl.BlockSpec((block, NY, NX), lambda i: (i, 0, 0)),
+    )(out)
 
 
 def solution(mesh):

time: 41.1 us -> 41.8 us (1.017)
  Pallas kernels: 38.2 us -> 41.6 us
  local copies, waits for them, and re-layouts: 2.81 us -> 0 us
    pallas_call x0 -> x1, Pallas kernels: none -> 3.44 us  [on_device(): pl.pallas_call(turn, grid=(NZ // block,), out_shape=jax.ShapeDtypeStruct(...]
    transpose x1 -> x0, local copies, waits for them, and re-layouts: 2.81 us -> none  [on_device(): return jnp.transpose(out, (1, 0, 2))]
where the time goes in v4:
time: 41.8 us; the launch traced here: 41.6 us
  Pallas kernels  41.6 us (100%)
    pallas_call x1, Pallas kernels, on_device(): pl.pallas_call(functools.partial(kernel, dims), out_shape=jax.ShapeDtypeS...  38.2 us
    pallas_call x1, Pallas kernels, on_device(): pl.pallas_call(turn, grid=(NZ // block,), out_shape=jax.ShapeDtypeStruct(...  3.44 us

profile of v4, /device:TPU:19, one launch (start us, length us, event | category | flops | bytes accessed | tf_op | source)
XLA Modules:
  0.0 41.6 jit_solution(14040032058869773019)
XLA Ops:
  0.0 38.2 %shard_map.55.x_ref = f32[16,64,256]{2,1,0:T(8,128)} custom-call(f32[1,64,16,256]{3,2,1,0:T(8,128)} %obs_hbm.1, f32[64,16,256]{2,1,0:T(8,128)} %start_hbm.1, f32[1,31]{1,0:T(1,128)} %sz_ref.1, f32[1,7]{1,0:T(1,128)} %sy_ref.1, f32[1,7]{1,0:T(1,128)} %sx_ref.1), custom_call_target="tpu_custom_call" | custom-call | tf_op jit(solution)/shard_map/pallas_call | solution.py:379
  38.2 3.4 %shard_map.56 = f32[64,16,256]{2,1,0:T(8,128)} custom-call(f32[16,64,256]{2,1,0:T(8,128)} %shard_map.55.x_ref), custom_call_target="tpu_custom_call" | custom-call | tf_op jit(solution)/shard_map/pallas_call | solution.py:400

commit v5 on v3

--- a/solution.py
+++ b/solution.py
@@ -19,7 +19,7 @@
 
 
 def kernel(dims, obs_hbm, start_hbm, sz_ref, sy_ref, sx_ref, out_hbm,
-           raw_z, raw_y, raw_x, stage, obs_z, obs_t, mine, theirs, wf, wb, tx, zbuf, ybuf, qbuf,
+           raw_z, raw_y, raw_x, peer, stage, obs_z, obs_t, mine, theirs, wf, wb, tx, zbuf, ybuf, qbuf,
            ebuf, cbuf, rybuf, rzbuf, lsem, osem, ssem, rsem, xssem, xrsem):
     NH, NY, NX, HZ, KZ, KY, KX, S, G = dims
     my, mz, mx = KY // 2, KZ // 2, KX // 2
@@ -348,15 +348,21 @@
                 update(p)
                 r0, rows_ = ROWS[p]
                 src = zbuf.at[pl.ds(r0, rows_), pl.ds(0, NH)]
-                dst = out_hbm.at[pl.ds(r0 - my, rows_), pl.ds(v * NH, NH)]
-                outs.append(pltpu.make_async_copy(src, dst, osem.at[n]))
                 outs.append(pltpu.make_async_remote_copy(
-                    src_ref=src, dst_ref=dst, send_sem=xssem.at[2 + n], recv_sem=xrsem.at[2 + n],
+                    src_ref=src, dst_ref=peer.at[pl.ds(r0 - my, rows_)],
+                    send_sem=xssem.at[2 + n], recv_sem=xrsem.at[2 + n],
                     device_id=partner, device_id_type=MESH))
                 outs[-1].start()
-                outs[-2].start()
+            stage[1] = jnp.transpose(zbuf[my:my + NY, 0:NH, :], (1, 0, 2))
+            save = pltpu.make_async_copy(stage.at[1], out_hbm.at[pl.ds(v * NH, NH)], osem.at[0])
+            save.start()
             for out in outs:
                 out.wait()
+            stage[2] = jnp.transpose(peer[...], (1, 0, 2))
+            save2 = pltpu.make_async_copy(stage.at[2], out_hbm.at[pl.ds((1 - v) * NH, NH)], osem.at[1])
+            save2.start()
+            save.wait()
+            save2.wait()
     for it in range(ITERS):
         sent(it, gz, gyc)
         sent(it, sz, sy)
@@ -374,12 +380,12 @@
     hbm = pl.BlockSpec(memory_space=pltpu.HBM)
     out = pl.pallas_call(
         functools.partial(kernel, dims),
-        out_shape=jax.ShapeDtypeStruct((NY, NZ, NX), F32),
+        out_shape=jax.ShapeDtypeStruct((NZ, NY, NX), F32),
         in_specs=[hbm] * 5,
         out_specs=hbm,
         scratch_shapes=[
             vm((1, KZ), F32), vm((1, KY), F32), vm((1, KX), F32),
-            vm((1, NH, NY, NX), F32), vm((2, NH, NY, NX), F32), vm((2, NY, NH, NX), F32),
+            vm((NY, NH, NX), F32), vm((3, NH, NY, NX), F32), vm((2, NH, NY, NX), F32), vm((2, NY, NH, NX), F32),
             vm((8, 128), F32), vm((8, 128), F32),
             vm((NE, 3 * NE), BF16), vm((NE, 3 * NE), BF16), vm((2, 2, 2, NX, NX), BF16),
             vm((NR, NE, NX), F32), vm((2, NY // 2 * NH, NX), BF16), vm((NY + 4 * my, NE, NX), F32),
@@ -392,7 +398,7 @@
         compiler_params=pltpu.CompilerParams(
             collective_id=0, has_side_effects=True, vmem_limit_bytes=67043328),
     )(observed, start, spread_z, spread_y, spread_x)
-    return jnp.transpose(out, (1, 0, 2))
+    return out
 
 
 def solution(mesh):

time: 41.1 us -> 41.3 us (level)
  Pallas kernels: 38.2 us -> 38.9 us
  local copies, waits for them, and re-layouts: 2.81 us -> 2.26 us
    transpose x1 -> x0, local copies, waits for them, and re-layouts: 2.81 us -> none  [on_device(): return jnp.transpose(out, (1, 0, 2))]
    unnamed x0 -> x1, local copies, waits for them, and re-layouts: none -> 2.26 us
    pallas_call x1, Pallas kernels: 38.2 us -> 38.9 us  [on_device(): pl.pallas_call(functools.partial(kernel, dims), out_shape=jax.ShapeDtypeS...]
where the time goes in v5:
time: 41.3 us; the launch traced here: 41.2 us
  Pallas kernels  38.9 us (94%)
  local copies, waits for them, and re-layouts  2.26 us (5%)
    pallas_call x1, Pallas kernels, on_device(): pl.pallas_call(functools.partial(kernel, dims), out_shape=jax.ShapeDtypeS...  38.9 us
    unnamed x1, local copies, waits for them, and re-layouts  2.26 us

profile of v5, /device:TPU:19, one launch (start us, length us, event | category | flops | bytes accessed | tf_op | source)
XLA Modules:
  0.0 41.2 jit_solution(3336031108936449686)
XLA Ops:
  0.0 38.9 %shard_map.55 = f32[64,16,256]{2,1,0:T(8,128)} custom-call(f32[1,64,16,256]{3,2,1,0:T(8,128)} %obs_hbm.1, f32[64,16,256]{2,1,0:T(8,128)} %start_hbm.1, f32[1,31]{1,0:T(1,128)} %sz_ref.1, f32[1,7]{1,0:T(1,128)} %sy_ref.1, f32[1,7]{1,0:T(1,128)} %sx_ref.1), custom_call_target="tpu_custom_call" | custom-call | tf_op jit(solution)/shard_map/pallas_call | solution.py:381
  38.9 2.3 %copy.7 = f32[64,16,256]{2,1,0:T(8,128)} copy(f32[64,16,256]{2,1,0:T(8,128)} %shard_map.55) | data formatting | bytes 2097152
